TPU v7x, 256 devices: a whole 4x4x8 slice. The times are simulated.
256 devices in a mesh: stream: 2 (over z_hi), dp: 16 (over x, y), tensor: 8 (over z_lo, core).
Axes of the slice: x: 4, y: 4, z: 8 (z_hi: 2, z_lo: 4; z = z_hi * 4 + z_lo), core: 2. Of those that a mesh axis runs over, the one named last changes fastest.
Arguments:
- hidden: bfloat16 [2, 256, 8192], P('stream', 'tensor', 'dp'), may hold values from -3 to 3
- cached_rotated_keys: bfloat16 [2, 256, 8, 256, 128], P('stream', 'dp', 'tensor'), may hold values from -6 to 6
- cached_values: bfloat16 [2, 256, 8, 256, 128], P('stream', 'dp', 'tensor'), may hold values from -18 to 18
- cache_lengths: int32 [2, 256], P('stream', 'dp'), may hold values from 1 to 256, as said below
- recent_ids: int32 [256, 128], replicated, may hold values from 0 to 65535
- guidance: float32 [256], replicated, may hold values from 1 to 3
- w_query: bfloat16 [8192, 8192], P('dp', 'tensor'), may hold values from -0.0625 to 0.0625
- key_value_weight: bfloat16 [8192, 2, 1024], P('dp', None, 'tensor'), may hold values from -0.0625 to 0.0625
- w_output: bfloat16 [8192, 8192], P('tensor', 'dp'), may hold values from -0.0625 to 0.0625
- norm_gain: bfloat16 [8192], P('dp'), may hold values from 0.5 to 1.5
- w_head: bfloat16 [8192, 65536], P(None, ('dp', 'tensor')), may hold values from -0.16503906 to 0.16503906
Outputs:
- guided_logprobs: float32 [256, 65536], P('stream', ('dp', 'tensor'))
Inputs may be any that keep to these rules, and one draw needn't show every extreme that they name: `cache_lengths`: every prompt has 1 to 256 filled slots in each stream; some prompt has all 256; lengths differ widely from one group of 16 prompts to the next.
All inputs are finite; a program needn't handle non-finite values.
Results may differ from a plain program's by a relative error of at most 0.0025.
Values may be sent and summed in bfloat16 or wider, within the bound.
A program may use at most 64 MiB of HBM per device.

v0:
```python
import jax
import jax.numpy as jnp
from jax import lax
from jax.sharding import PartitionSpec as P

MODEL_WIDTH = 8192
HEAD_SIZE = 128


rope_theta = 500000.0
penalty_step = 1.5
norm_eps = 1e-05


def partner_2(value, axis, distance):
    mask = 2**distance
    pairs = [(source, source ^ mask) for source in range(lax.axis_size(axis))]
    return lax.ppermute(value, axis, pairs)


def rotate(values, positions):
    halfway = values.shape[-1] // 2
    frequency = rope_theta ** (-(jnp.arange(halfway, dtype=jnp.float32) * 2.0 / values.shape[-1]))
    angles = positions.astype(jnp.float32)[:, None, None] * frequency
    cosine_term = jnp.cos(angles)
    sine_term = jnp.sin(angles)
    first_half = values[..., :halfway]
    second_half = values[..., halfway:]
    return jnp.concatenate(
        [
            first_half * cosine_term - second_half * sine_term,
            second_half * cosine_term + first_half * sine_term,
        ],
        axis=-1,
    )


def repeat_counts(recent_ids, first_column, width):
    columns = first_column + jnp.arange(width, dtype=jnp.int32)
    return jnp.sum((recent_ids[:, :, None] == columns[None, None, :]).astype(jnp.float32), 1)


def body(
    hidden,
    cached_rotated_keys,
    cached_values,
    cache_lengths,
    recent_ids,
    guidance,
    w_query,
    key_value_weight,
    w_output,
    norm_gain,
    w_head,
):
    local_width = hidden.shape[2]
    query_cols = w_query.shape[1]
    kv_cols = key_value_weight.shape[2]
    local_prompts = cache_lengths.shape[1]
    lengths = cache_lengths[0]
    vocab_local = w_head.shape[1]
    all_rows = lax.all_gather(hidden[0], "tensor", axis=0, tiled=True)
    kv_flat = key_value_weight.reshape(local_width, 2 * kv_cols)
    projected = lax.psum_scatter(
        jnp.concatenate(
            [
                jnp.dot(all_rows, w_query, preferred_element_type=jnp.float32),
                jnp.dot(all_rows, kv_flat, preferred_element_type=jnp.float32),
            ],
            axis=1,
        ),
        "dp",
        scatter_dimension=0,
        tiled=True,
    )
    query_heads = query_cols // HEAD_SIZE
    kv_heads = kv_cols // HEAD_SIZE
    rotated_query = rotate(
        projected[:, :query_cols].reshape(local_prompts, query_heads, HEAD_SIZE), lengths
    ).astype(jnp.bfloat16)
    key_value_rows = projected[:, query_cols:].reshape(local_prompts, 2, kv_heads, HEAD_SIZE)
    fresh_key = rotate(key_value_rows[:, 0], lengths).astype(jnp.bfloat16)
    value_new = key_value_rows[:, 1].astype(jnp.bfloat16)
    grouped_queries = rotated_query.reshape(
        local_prompts, kv_heads, query_heads // kv_heads, HEAD_SIZE
    )
    attention_scale = HEAD_SIZE ** (-0.5)
    key_block = cached_rotated_keys[0]
    value_block = cached_values[0]
    scores = (
        jnp.einsum(
            "pkgd,pksd->pkgs", grouped_queries, key_block, preferred_element_type=jnp.float32
        )
        * attention_scale
    )
    self_score = (
        jnp.einsum("pkgd,pkd->pkg", grouped_queries, fresh_key, preferred_element_type=jnp.float32)
        * attention_scale
    )
    valid = jnp.arange(key_block.shape[2], dtype=jnp.int32)[None, :] < lengths[:, None]
    exps = jnp.where(valid[:, None, None, :], jnp.exp(scores), 0.0)
    own_exp = jnp.exp(self_score)
    denominator = jnp.sum(exps, -1) + own_exp
    weights = (exps / denominator[..., None]).astype(jnp.bfloat16)
    own_weight = (own_exp / denominator).astype(jnp.bfloat16)
    attended = jnp.einsum(
        "pkgs,pksd->pkgd", weights, value_block, preferred_element_type=jnp.float32
    )
    attended = (
        attended
        + own_weight.astype(jnp.float32)[..., None] * value_new.astype(jnp.float32)[:, :, None, :]
    )
    attended = attended.reshape(local_prompts, query_cols).astype(jnp.bfloat16)
    partial_out = jnp.dot(
        lax.all_gather(attended, "dp", axis=0, tiled=True),
        w_output,
        preferred_element_type=jnp.float32,
    )
    output_sum = lax.psum_scatter(partial_out, "tensor", scatter_dimension=0, tiled=True)
    residual = (hidden[0].astype(jnp.float32) + output_sum).astype(jnp.bfloat16)
    widened = residual.astype(jnp.float32)
    squares = lax.psum(jnp.sum(widened * widened, 1), "dp")
    inverse = lax.rsqrt(squares / MODEL_WIDTH + norm_eps)
    normed = (widened * inverse[:, None] * norm_gain.astype(jnp.float32)).astype(jnp.bfloat16)
    normed_all = lax.all_gather(normed, "tensor", axis=0, tiled=True)
    logits = jnp.dot(
        lax.all_gather(normed_all, "dp", axis=1, tiled=True),
        w_head,
        preferred_element_type=jnp.float32,
    )
    stream_side = lax.axis_index("stream")
    half_rows = logits.shape[0] // 2
    mine_start = stream_side * half_rows
    other_start = (1 - stream_side) * half_rows
    column_base = lax.axis_index(("dp", "tensor")) * vocab_local
    mine = lax.dynamic_slice_in_dim(logits, mine_start, half_rows, 0)
    sending = lax.dynamic_slice_in_dim(logits, other_start, half_rows, 0)
    partner = partner_2(sending, "stream", 0)
    conditional = jnp.where(stream_side == 0, mine, partner)
    unconditional = jnp.where(stream_side == 0, partner, mine)
    guide = lax.dynamic_slice_in_dim(guidance, mine_start, half_rows, 0)[:, None]
    recent_mine = lax.dynamic_slice_in_dim(recent_ids, mine_start, half_rows, 0)
    guided = unconditional + guide * (conditional - unconditional)
    guided = guided - penalty_step * repeat_counts(recent_mine, column_base, vocab_local)
    totals = lax.psum(jnp.sum(jnp.exp(guided), 1), ("dp", "tensor"))
    return guided - jnp.log(totals)[:, None]


def solution(mesh):
    return jax.shard_map(
        body,
        mesh=mesh,
        in_specs=(
            P("stream", "tensor", "dp"),
            P("stream", "dp", "tensor", None, None),
            P("stream", "dp", "tensor", None, None),
            P("stream", "dp"),
            P(),
            P(),
            P("dp", "tensor"),
            P("dp", None, "tensor"),
            P("tensor", "dp"),
            P("dp"),
            P(None, ("dp", "tensor")),
        ),
        out_specs=P("stream", ("dp", "tensor")),
        check_vma=False,
    )
```

profile of v0, /device:TPU:1, one launch (start us, length us, event | category | flops | bytes accessed | tf_op | source)
XLA Modules:
  0.0 645.8 jit_solution(1154850240006349418)
XLA Ops:
  6.6 17.6 %all-gather = bf16[1,256,512]{2,1,0:T(8,128)(2,1)S(1)} all-gather(bf16[1,32,512]{2,1,0:T(8,128)(2,1)} %param.11), channel_id=2, replica_groups=mesh['stream'=2,'dp'=16,'tensor'=8] {'tensor'}, dimensions={1}, use_global_device_ids=true | all-gather | bytes 294912 | tf_op jit(solution)/shard_map/all_gather | solution.py:62
  24.2 0.5 fusion.9
  24.7 1.2 fusion.5
  25.9 1.2 pad_maximum_fusion
  27.1 0.7 bitcast_convert_fusion
  27.8 0.7 iota_compare_fusion
  28.6 76.8 %reduce-scatter.3.cloned.1.call-done = f32[16,1280]{1,0:T(8,128)} async-done(((f32[256,1280]{1,0:T(8,128)}), f32[16,1280]{1,0:T(8,128)}) %reduce-scatter.3.cloned.1.call-update) | async-done | bytes 81936 | tf_op jit(solution)/shard_map/reduce_scatter | solution.py:64
  105.4 0.7 slice.36
  106.3 0.8 slice_bitcast_fusion
  107.5 1.7 fusion.33
  109.3 0.3 fusion.2
  109.7 17.2 %all_gather.13 = bf16[256,1024]{1,0:T(8,128)(2,1)S(1)} all-gather(bf16[16,1024]{1,0:T(8,128)(2,1)S(1)} %bitcast.51), channel_id=1, replica_groups=mesh['stream'=2,'dp'=16,'tensor'=8] {'dp'}, dimensions={0}, use_global_device_ids=true | all-gather | bytes 557056 | tf_op jit(solution)/shard_map/all_gather | solution.py:115
  126.8 1.2 fusion.34
  128.1 40.3 %reduce-scatter.5.cloned.1.call-done = f32[32,512]{1,0:T(8,128)} async-done(((f32[256,512]{1,0:T(8,128)}), f32[32,512]{1,0:T(8,128)}) %reduce-scatter.5.cloned.1.call-update) | async-done | bytes 65552 | tf_op jit(solution)/shard_map/reduce_scatter | solution.py:119
  168.4 1.0 fusion.11
  169.4 33.3 %psum.14 = f32[32]{0:T(128)S(1)} all-reduce(f32[32]{0:T(128)S(1)} %fusion.11), channel_id=1, replica_groups=mesh['stream'=2,'dp'=16,'tensor'=8] {'dp'}, use_global_device_ids=true, to_apply=%region_4.5 | all-reduce | flops 32 | bytes 256 | tf_op jit(solution)/shard_map/psum | solution.py:122
  202.7 0.9 fusion.13
  203.7 25.8 %all_gather.14 = bf16[256,512]{1,0:T(8,128)(2,1)} all-gather(bf16[32,512]{1,0:T(8,128)(2,1)S(1)} %fusion.13), channel_id=1, replica_groups=mesh['stream'=2,'dp'=16,'tensor'=8] {'tensor'}, dimensions={0}, use_global_device_ids=true | all-gather | bytes 294912 | tf_op jit(solution)/shard_map/all_gather | solution.py:125
  229.6 53.8 %all-gather.3.cloned.1.call-done = bf16[256,8192]{1,0:T(8,128)(2,1)} async-done(((bf16[256,512]{1,0:T(8,128)(2,1)}), bf16[256,8192]{1,0:T(8,128)(2,1)}) %all-gather.3.cloned.1.call-update) | async-done | bytes 4194320 | tf_op jit(solution)/shard_map/all_gather | solution.py:127
  283.4 7.0 %fusion.35 = f32[256,512]{1,0:T(8,128)S(1)} fusion(bf16[256,8192]{1,0:T(8,128)(2,1)} %all-gather.3.cloned.1.call-done, bf16[8192,512]{1,0:T(8,128)(2,1)} %param.21), kind=kOutput, calls=%fused_computation.66 | convolution fusion | flops 2147483648 | bytes 13107200 | tf_op jit(solution)/shard_map/dot_general | solution.py:126
  290.4 5.5 collective-permute-start
  295.9 4.7 convert_reduce_fusion
  300.8 337.6 %psum.15 = f32[128]{0:T(128)S(1)} all-reduce(f32[128]{0:T(128)S(1)} %get-tuple-element.5), channel_id=1, replica_groups=mesh['stream'=2,'dp'=16,'tensor'=8] {'dp','tensor'}, use_global_device_ids=true, to_apply=%region_7.8 | all-reduce | flops 128 | bytes 1024 | tf_op jit(solution)/shard_map/psum | solution.py:145
  638.5 0.8 broadcast_subtract_fusion
  (41 shorter events, 1.3 us)
Async XLA Ops:
  6.5 17.7 %copy-start = (bf16[512,1024]{1,0:T(8,128)(2,1)S(1)}, bf16[512,1024]{1,0:T(8,128)(2,1)}, u32[]{:S(2)}) copy-start(bf16[512,1024]{1,0:T(8,128)(2,1)} %param.17) | copy-start | bytes 3145732
  6.5 161.9 %copy-start.3 = (bf16[1,32,512]{2,1,0:T(8,128)(2,1)S(1)}, bf16[1,32,512]{2,1,0:T(8,128)(2,1)}, u32[]{:S(2)}) copy-start(bf16[1,32,512]{2,1,0:T(8,128)(2,1)} %param.11) | copy-start | bytes 98308
  6.5 102.8 %copy-start.1 = (bf16[1,16,1,256,128]{4,3,2,1,0:T(8,128)(2,1)S(1)}, bf16[1,16,1,256,128]{4,3,2,1,0:T(8,128)(2,1)}, u32[]{:S(2)}) copy-start(bf16[1,16,1,256,128]{4,3,2,1,0:T(8,128)(2,1)} %param.13) | copy-start | bytes 3145732
  6.5 120.3 %copy-start.2 = (bf16[1024,512]{1,0:T(8,128)(2,1)S(1)}, bf16[1024,512]{1,0:T(8,128)(2,1)}, u32[]{:S(2)}) copy-start(bf16[1024,512]{1,0:T(8,128)(2,1)} %param.19) | copy-start | bytes 3145732
  6.5 121.6 %copy-start.5 = (bf16[512]{0:T(512)(128)(2,1)S(1)}, bf16[512]{0:T(512)(128)(2,1)}, u32[]{:S(2)}) copy-start(bf16[512]{0:T(512)(128)(2,1)} %param.20) | copy-start | bytes 3076
  6.5 222.9 %copy-start.6 = (f32[256]{0:T(256)S(1)}, f32[256]{0:T(256)}, u32[]{:S(2)}) copy-start(f32[256]{0:T(256)} %param.16) | copy-start | bytes 3076
  6.6 223.0 %copy-start.4 = (s32[256,128]{1,0:T(8,128)S(1)}, s32[256,128]{1,0:T(8,128)}, u32[]{:S(2)}) copy-start(s32[256,128]{1,0:T(8,128)} %param.15) | copy-start | bytes 393220
  6.6 98.8 %reduce-scatter.3.cloned.1.call-start = ((), (), s32[]{:S(2)}) async-start(), calls=%async_computation.2 | async-start | bytes 1392640 | tf_op jit(solution)/shard_map/reduce_scatter | solution.py:64
  27.0 141.4 %reduce-scatter.5.cloned.1.call-start = ((), (), s32[]{:S(2)}) async-start(), calls=%async_computation.3 | async-start | bytes 589824 | tf_op jit(solution)/shard_map/reduce_scatter | solution.py:119
  128.1 155.3 %all-gather.3.cloned.1.call-start = ((), (), s32[]{:S(2)}) async-start(), calls=%async_computation.4 | async-start | bytes 4456448 | tf_op jit(solution)/shard_map/all_gather | solution.py:127
  290.4 10.2 %collective-permute-start = (f32[128,512]{1,0:T(8,128)S(1)}, f32[128,512]{1,0:T(8,128)S(1)}, u32[]{:S(2)}, u32[]{:S(2)}) collective-permute-start(f32[128,512]{1,0:T(8,128)S(1)} %constant_dynamic-slice_fusion.1), channel_id=1, source_target_pairs={{0,128},{128,0},{1,129},{129,1},{2,130},{130,2},{3,131},{131,3},{4... | collective-permute-start | bytes 786440 | tf_op jit(solution)/shard_map/ppermute | solution.py:18
Sparse Core Ops, SparseCore 0:
  27.2 78.2 reduce-scatter.2
  128.2 40.1 reduce-scatter.4
  229.6 53.7 all-gather.2
where the time goes:
time: 648 us; the launch traced here: 646 us
  blocking collectives  432 us (67%)
  waiting for transfers between devices  171 us (26%)
  between operations  13.3 us (2%)
  matrix products  12.1 us (2%)
  other arithmetic  10.6 us (2%)
    psum x1, blocking collectives, body(): totals = lax.psum(jnp.sum(jnp.exp(guided), 1), ('dp', 'tensor'))  338 us
    reduce_scatter x1, waiting for transfers between devices, body(): lax.psum_scatter(jnp.concatenate([jnp.dot(all_rows, w_query, preferred_el...  76.8 us
    all_gather x1, waiting for transfers between devices, body(): lax.all_gather(normed_all, 'dp', axis=1, tiled=True)  53.8 us
    reduce_scatter x1, waiting for transfers between devices, body(): lax.psum_scatter(partial_out, 'tensor', scatter_dimension=0, tiled=True)  40.3 us
    psum x1, blocking collectives, body(): squares = lax.psum(jnp.sum(widened * widened, 1), 'dp')  33.3 us
    all_gather x1, blocking collectives, body(): normed_all = lax.all_gather(normed, 'tensor', axis=0, tiled=True)  25.8 us
    all_gather x1, blocking collectives, body(): all_rows = lax.all_gather(hidden[0], 'tensor', axis=0, tiled=True)  17.6 us
    all_gather x1, blocking collectives, body(): lax.all_gather(attended, 'dp', axis=0, tiled=True)  17.2 us
  transfers between devices with their start and end apart: 4, of which 3 were waited for; matrix products, arithmetic and copies ran while one was open for 1% of the time, Pallas kernels for 0%

commit v1 on v0

v1 whole, which is shorter than its diff:
```python
import jax
import jax.numpy as jnp
from jax import lax
from jax.experimental import pallas as pl
from jax.experimental.pallas import tpu as pltpu
from jax.sharding import PartitionSpec as P

MESH = pl.DeviceIdType.MESH
F32 = jnp.float32
BF16 = jnp.bfloat16
WIDTH = 8192
HEAD = 128
RING = 4
DP = 16
TEN = 8

rope_theta = 500000.0
penalty_step = 1.5
norm_eps = 1e-05


def routes():
    found = []
    for depth in range(5):
        for dx in range(RING):
            for dy in range(RING):
                if min(dx, RING - dx) + min(dy, RING - dy) != depth:
                    continue
                for quarter in range(4):
                    first, second = (dx, dy) if quarter < 2 else (dy, dx)
                    names = ("x", "y") if quarter < 2 else ("y", "x")
                    odd = quarter % 2
                    hops = []
                    if second == 0:
                        if first == 0:
                            hops += [(names[0], 1), (names[0], -1)]
                        elif first == 1 and not odd:
                            hops += [(names[0], 1)]
                        elif first == 3 and odd:
                            hops += [(names[0], -1)]
                        hops += [(names[1], 1), (names[1], -1)]
                    elif second == 1 and not odd:
                        hops += [(names[1], 1)]
                    elif second == 3 and odd:
                        hops += [(names[1], -1)]
                    found.append((depth, dx, dy, quarter, hops))
    return found


ROUTES = routes()
N_FORWARD = sum(len(r[4]) for r in ROUTES)
OFFSETS = [
    sorted({(r[1], r[2]) for r in ROUTES if r[0] == depth}) for depth in range(5)
]


def kernel(
    hidden,
    keys,
    vals,
    lens,
    ids,
    guid,
    wq,
    kvw,
    wo,
    gain,
    wh,
    out,
    h_all,
    wq_v,
    kvw_v,
    k_v,
    v_v,
    wo_v,
    wh_v,
    ids_v,
    gain_all,
    part,
    recv_b,
    q_s,
    att_s,
    att_all,
    part_d,
    recv_d,
    resid,
    buf,
    acc,
    ssq,
    counts,
    gcol,
    tot_one,
    tot_t,
    tot_d,
    load_sem,
    a_send,
    a_recv,
    gain_send,
    gain_recv,
    b_send,
    b_recv,
    c_send,
    c_recv,
    d_send,
    d_recv,
    z_send,
    z_recv,
    f_send,
    f_recv,
    sib_send,
    sib_recv,
    t_send,
    t_recv,
    s_send,
    s_recv,
):
    S = lax.axis_index("stream")
    D = lax.axis_index("dp")
    T = lax.axis_index("tensor")
    zl, c = T // 2, T % 2
    x, y = D // RING, D % RING
    sib = (S, D, zl * 2 + 1 - c)

    def remote(src, dst, ssem, rsem, dev):
        copy = pltpu.make_async_remote_copy(
            src_ref=src,
            dst_ref=dst,
            send_sem=ssem,
            recv_sem=rsem,
            device_id=dev,
            device_id_type=MESH,
        )
        copy.start()
        return copy

    def arrived(ref, rsem, ssem):
        pltpu.make_async_remote_copy(
            src_ref=ref,
            dst_ref=ref,
            send_sem=ssem,
            recv_sem=rsem,
            device_id=sib,
            device_id_type=MESH,
        ).wait_recv()

    sent = []

    barrier = pltpu.get_barrier_semaphore()
    for i in range(1, DP):
        pl.semaphore_signal(
            barrier, inc=1, device_id=(S, (D + i) % DP, T), device_id_type=MESH
        )
    for i in range(1, 16):
        other = (S * TEN + T + i) % 16
        pl.semaphore_signal(
            barrier, inc=1, device_id=(other // TEN, D, other % TEN), device_id_type=MESH
        )

    loads = []

    def load(src, dst):
        copy = pltpu.make_async_copy(src, dst, load_sem.at[len(loads)])
        copy.start()
        loads.append(copy)
        return copy

    l_h = load(hidden.at[0], h_all.at[T])
    l_wq = load(wq, wq_v)
    l_kv = load(kvw, kvw_v)
    l_ids = load(ids.at[pl.ds(S * 128, 128), :], ids_v)
    l_k = load(keys.at[0, :, 0], k_v)
    l_v = load(vals.at[0, :, 0], v_v)
    l_wo = load(wo, wo_v)
    pl.semaphore_wait(barrier, 30)

    for dz in (3, 2, 1):
        dev = (S, D, ((zl + dz) % 4) * 2 + c)
        sent.append(remote(hidden.at[0], h_all.at[T], a_send.at[dz], a_recv.at[T], dev))
    sent.append(remote(hidden.at[0], h_all.at[T], a_send.at[0], a_recv.at[T], sib))
    gain_row = gain[...].astype(F32)
    gain_all[D] = gain_row
    l_wh = load(wh, wh_v)
    for n, dz in enumerate((1, 3, 2)):
        src = ((zl + dz) % 4) * 2 + c
        arrived(h_all.at[src], a_recv.at[src], a_send.at[0])
        sent.append(remote(h_all.at[src], h_all.at[src], a_send.at[4 + n], a_recv.at[src], sib))
    l_h.wait()
    l_wq.wait()
    l_kv.wait()
    for dz in range(4):
        src = ((zl + dz) % 4) * 2 + 1 - c
        arrived(h_all.at[src], a_recv.at[src], a_send.at[0])

    h = h_all[...].reshape(256, 512)
    for n in range(4):
        cols = pl.ds(n * 256, 256)
        r = jnp.dot(h, wq_v[:, cols], preferred_element_type=F32)
        part[:, :, cols] = r.reshape(DP, 16, 256).astype(BF16)
    for n in range(2):
        cols = pl.ds(1024 + n * 128, 128)
        r = jnp.dot(h, kvw_v[:, n, :], preferred_element_type=F32)
        part[:, :, cols] = r.reshape(DP, 16, 128).astype(BF16)
    for i in range(1, DP):
        to = (D + i) % DP
        sent.append(remote(part.at[to], recv_b.at[D], b_send.at[i], b_recv.at[D], (S, to, T)))
    for i in range(1, DP):
        to = (D + i) % DP
        sent.append(
            remote(gain_all.at[D], gain_all.at[D], gain_send.at[i], gain_recv.at[D], (S, to, T))
        )

    lane = lax.broadcasted_iota(jnp.int32, (16, HEAD), 1)
    row = lax.broadcasted_iota(jnp.int32, (16, HEAD), 0)
    freq = jnp.exp(((lane % 64).astype(F32) * (2.0 / HEAD)) * (-jnp.log(F32(rope_theta))))
    position = jnp.zeros((16, HEAD), jnp.int32)
    for p in range(16):
        position = jnp.where(row == p, lens[0, p], position)
    angle = position.astype(F32) * freq
    cosine = jnp.cos(angle)
    sine = jnp.sin(angle) * jnp.where(lane < 64, -1.0, 1.0)

    l_ids.wait()
    base = (D * TEN + T) * 512
    ids_v[...] = jnp.transpose(ids_v[...]) - base
    for n in range(4):
        column = lax.broadcasted_iota(jnp.int32, (128, 128), 0) + n * 128

        def add(r, total):
            for k in range(8):
                here = ids_v[pl.ds(r * 8 + k, 1), :]
                total = total + jnp.where(column == here, 1.0, 0.0)
            return total

        total = lax.fori_loop(0, 16, add, jnp.zeros((128, 128), F32))
        counts[:, pl.ds(n * 128, 128)] = jnp.transpose(total) * penalty_step
    gcol[...] = jnp.transpose(jnp.broadcast_to(guid[pl.ds(S, 1), :], (128, 128)))

    qkv = part[D].astype(F32)
    for i in range(1, DP):
        src = (D + DP - i) % DP
        arrived(recv_b.at[src], b_recv.at[src], b_send.at[i])
        qkv = qkv + recv_b[src].astype(F32)

    def turn(v):
        return v * cosine + pltpu.roll(v, 64, 1) * sine

    for g in range(8):
        q_s[:, g, :] = turn(qkv[:, g * HEAD : (g + 1) * HEAD])
    k_new = turn(qkv[:, 1024:1152]).astype(BF16).astype(F32)
    v_new = qkv[:, 1152:1280].astype(BF16).astype(F32)

    l_k.wait()
    l_v.wait()
    scale = HEAD ** (-0.5)
    slot_at = lax.broadcasted_iota(jnp.int32, (8, 256), 1)
    for p in range(16):
        q = q_s[p].astype(BF16)
        scores = (
            lax.dot_general(q, k_v[p], (((1,), (1,)), ((), ())), preferred_element_type=F32)
            * scale
        )
        own = jnp.sum(q.astype(F32) * k_new[p : p + 1, :], axis=1, keepdims=True) * scale
        e = jnp.where(slot_at < lens[0, p], jnp.exp(scores), 0.0)
        e_own = jnp.exp(own)
        den = jnp.sum(e, axis=1, keepdims=True) + e_own
        w = (e / den).astype(BF16)
        w_own = (e_own / den).astype(BF16).astype(F32)
        o = jnp.dot(w, v_v[p], preferred_element_type=F32) + w_own * v_new[p : p + 1, :]
        att_s[p] = o
    for g in range(8):
        att_all[D, :, pl.ds(g * HEAD, HEAD)] = att_s[:, g, :].astype(BF16)

    def neighbour(name, step):
        if name == "x":
            return (S, ((x + RING + step) % RING) * RING + y, T)
        return (S, x * RING + (y + RING + step) % RING, T)

    def gather(depth, view, send, recv, count, each=None):
        for level, dx, dy, quarter, hops in ROUTES:
            if level != depth:
                continue
            slot = ((x + RING - dx) % RING) * RING + (y + RING - dy) % RING
            piece = view(slot, quarter)
            if depth > 0:
                arrived(piece, recv.at[slot, quarter], send.at[0])
            for hop in hops:
                sent.append(
                    remote(piece, piece, send.at[count], recv.at[slot, quarter], neighbour(*hop))
                )
                count += 1
            if each is not None:
                each(slot, quarter)
        return count

    done = 0
    for depth in range(5):
        done = gather(
            depth,
            lambda slot, quarter: att_all.at[slot, :, pl.ds(quarter * 256, 256)],
            c_send,
            c_recv,
            done,
        )

    l_wo.wait()
    a = att_all[...].reshape(256, 1024)
    for n in range(2):
        cols = pl.ds(n * 256, 256)
        r = jnp.dot(a, wo_v[:, cols], preferred_element_type=F32)
        part_d[:, :, cols] = r.reshape(TEN, 32, 256).astype(BF16)

    def owned(t):
        inner = ((t + 2) // 4) % 2
        half = inner * S + (1 - inner) * (1 - S)
        return half, inner * (t - 2) + (1 - inner) * (t - 4 * (t // 6))

    for i in range(1, TEN):
        to = (T + i) % TEN
        half, j = owned(to)
        sent.append(
            remote(part_d.at[half * 4 + j], recv_d.at[T], d_send.at[i], d_recv.at[T], (S, D, to))
        )
    my_half, my_j = owned(T)
    mine = my_half * 4 + my_j
    total = h_all[mine].astype(F32) + part_d[mine].astype(F32)
    for i in range(1, TEN):
        src = (T + TEN - i) % TEN
        arrived(recv_d.at[src], d_recv.at[src], d_send.at[i])
        total = total + recv_d[src].astype(F32)
    resid[...] = total.astype(BF16)

    place = buf.at[S, D, pl.ds(my_j * 32, 32), :]
    for z in range(4):
        at_home = jnp.logical_and(my_half == S, 2 * z + S == T)

        @pl.when(at_home)
        def _():
            pltpu.make_async_copy(resid, place, z_recv.at[my_j]).start()

        @pl.when(jnp.logical_not(at_home))
        def _():
            remote(resid, place, z_send.at[z], z_recv.at[my_j], (my_half, D, 2 * z + S))

    for i in range(1, DP):
        src = (D + DP - i) % DP
        arrived(gain_all.at[src], gain_recv.at[src], gain_send.at[i])
    l_wh.wait()
    acc[...] = jnp.zeros_like(acc)
    ssq[...] = jnp.zeros_like(ssq)

    def rows(slot, quarter):
        return buf.at[c, slot, pl.ds(quarter * 32, 32), :]

    passed = [0]

    def share(slot, quarter):
        piece = rows(slot, quarter)
        sent.append(
            remote(piece, piece, sib_send.at[passed[0]], sib_recv.at[slot, quarter], sib)
        )
        passed[0] += 1

    def head(depth):
        offsets = OFFSETS[depth]

        def step(i, carry):
            dx, dy = jnp.int32(offsets[0][0]), jnp.int32(offsets[0][1])
            for n, (ox, oy) in enumerate(offsets[1:]):
                dx = jnp.where(i == n + 1, ox, dx)
                dy = jnp.where(i == n + 1, oy, dy)
            slot = ((x + RING - dx) % RING) * RING + (y + RING - dy) % RING
            for quarter in range(4):
                there = buf.at[1 - c, slot, pl.ds(quarter * 32, 32), :]
                arrived(there, sib_recv.at[slot, quarter], sib_send.at[0])
            v = buf[:, slot].reshape(256, 512).astype(F32)
            v2 = v * v
            ssq[...] += (
                v2[:, 0:128] + v2[:, 128:256] + v2[:, 256:384] + v2[:, 384:512]
            )
            w = (v * gain_all[slot]).astype(BF16)
            acc[...] += jnp.dot(
                w, wh_v[pl.ds(pl.multiple_of(slot * 512, 512), 512), :], preferred_element_type=F32
            )
            return carry

        lax.fori_loop(0, len(offsets), step, 0)

    for quarter in range(4):
        arrived(rows(D, quarter), z_recv.at[quarter], z_send.at[0])
    done = 0
    for depth in range(5):
        done = gather(depth, rows, f_send, f_recv, done, share)
        if depth > 0:
            head(depth - 1)
    head(4)

    inv = lax.rsqrt(jnp.sum(ssq[...], axis=1, keepdims=True) / WIDTH + norm_eps)
    cond = acc[0:128, :] * inv[0:128]
    uncond = acc[128:256, :] * inv[128:256]
    guide = gcol[:, 0:1]
    guided = uncond + guide * (cond - uncond) - counts[...]
    acc[0:128, :] = guided
    e = jnp.exp(guided)
    e = e[:, 0:128] + e[:, 128:256] + e[:, 256:384] + e[:, 384:512]
    tot_one[...] = jnp.sum(jnp.transpose(e), axis=0, keepdims=True)
    tot_t[T] = tot_one[...]
    for i in range(1, TEN):
        to = (T + i) % TEN
        sent.append(remote(tot_one, tot_t.at[T], t_send.at[i], t_recv.at[T], (S, D, to)))
    for i in range(1, TEN):
        src = (T + TEN - i) % TEN
        arrived(tot_t.at[src], t_recv.at[src], t_send.at[i])
    tot_d[D] = jnp.sum(tot_t[...], axis=0)
    for i in range(1, DP):
        to = (D + i) % DP
        sent.append(remote(tot_d.at[D], tot_d.at[D], s_send.at[i], s_recv.at[D], (S, to, T)))
    for i in range(1, DP):
        src = (D + DP - i) % DP
        arrived(tot_d.at[src], s_recv.at[src], s_send.at[i])
    log_total = jnp.transpose(jnp.broadcast_to(jnp.log(jnp.sum(tot_d[...], axis=0)), (128, 128)))
    for n in range(4):
        cols = pl.ds(n * 128, 128)
        out[:, cols] = acc[0:128, cols] - log_total

    for copy in sent:
        copy.wait_send()
    for z in range(4):
        at_home = jnp.logical_and(my_half == S, 2 * z + S == T)

        @pl.when(jnp.logical_not(at_home))
        def _():
            pltpu.make_async_remote_copy(
                src_ref=resid,
                dst_ref=place,
                send_sem=z_send.at[z],
                recv_sem=z_recv.at[my_j],
                device_id=(my_half, D, 2 * z + S),
                device_id_type=MESH,
            ).wait_send()


def body(hidden, keys, vals, lens, ids, guid, wq, kvw, wo, gain, wh):
    dma = pltpu.SemaphoreType.DMA
    anywhere = pl.BlockSpec(memory_space=pl.ANY)
    vmem = pl.BlockSpec(memory_space=pltpu.VMEM)
    smem = pl.BlockSpec(memory_space=pltpu.SMEM)
    return pl.pallas_call(
        kernel,
        out_shape=jax.ShapeDtypeStruct((128, 512), F32),
        in_specs=[
            anywhere,
            anywhere,
            anywhere,
            smem,
            anywhere,
            vmem,
            anywhere,
            anywhere,
            anywhere,
            vmem,
            anywhere,
        ],
        out_specs=vmem,
        scratch_shapes=[
            pltpu.VMEM((8, 32, 512), BF16),
            pltpu.VMEM((512, 1024), BF16),
            pltpu.VMEM((512, 2, 128), BF16),
            pltpu.VMEM((16, 256, 128), BF16),
            pltpu.VMEM((16, 256, 128), BF16),
            pltpu.VMEM((1024, 512), BF16),
            pltpu.VMEM((8192, 512), BF16),
            pltpu.VMEM((128, 128), jnp.int32),
            pltpu.VMEM((DP, 1, 512), F32),
            pltpu.VMEM((DP, 16, 1280), BF16),
            pltpu.VMEM((DP, 16, 1280), BF16),
            pltpu.VMEM((16, 8, 128), F32),
            pltpu.VMEM((16, 8, 128), F32),
            pltpu.VMEM((DP, 16, 1024), BF16),
            pltpu.VMEM((TEN, 32, 512), BF16),
            pltpu.VMEM((TEN, 32, 512), BF16),
            pltpu.VMEM((32, 512), BF16),
            pltpu.VMEM((2, DP, 128, 512), BF16),
            pltpu.VMEM((256, 512), F32),
            pltpu.VMEM((256, 128), F32),
            pltpu.VMEM((128, 512), F32),
            pltpu.VMEM((128, 128), F32),
            pltpu.VMEM((1, 128), F32),
            pltpu.VMEM((TEN, 1, 128), F32),
            pltpu.VMEM((DP, 1, 128), F32),
            dma((8,)),
            dma((8,)),
            dma((8,)),
            dma((DP,)),
            dma((DP,)),
            dma((DP,)),
            dma((DP,)),
            dma((N_FORWARD,)),
            dma((DP, 4)),
            dma((TEN,)),
            dma((TEN,)),
            dma((4,)),
            dma((4,)),
            dma((N_FORWARD,)),
            dma((DP, 4)),
            dma((64,)),
            dma((DP, 4)),
            dma((TEN,)),
            dma((TEN,)),
            dma((DP,)),
            dma((DP,)),
        ],
        compiler_params=pltpu.CompilerParams(
            collective_id=0, has_side_effects=True, vmem_limit_bytes=60 * 1024 * 1024
        ),
    )(hidden, keys, vals, lens, ids, guid.reshape(2, 128), wq, kvw, wo, gain.reshape(1, 512), wh)


def solution(mesh):
    return jax.shard_map(
        body,
        mesh=mesh,
        in_specs=(
            P("stream", "tensor", "dp"),
            P("stream", "dp", "tensor", None, None),
            P("stream", "dp", "tensor", None, None),
            P("stream", "dp"),
            P(),
            P(),
            P("dp", "tensor"),
            P("dp", None, "tensor"),
            P("tensor", "dp"),
            P("dp"),
            P(None, ("dp", "tensor")),
        ),
        out_specs=P("stream", ("dp", "tensor")),
        check_vma=False,
    )
```

time: 648 us -> 94.1 us (0.15)
  blocking collectives: 432 us -> 0 us
  waiting for transfers between devices: 171 us -> 0 us
  Pallas kernels: 0 us -> 91 us
  between operations: 13.3 us -> 0.01 us
  matrix products: 12.1 us -> 0 us
  other arithmetic: 10.6 us -> 0 us
    psum x2 -> x0, blocking collectives: 371 us -> none  [the longest x1 338 us: body(): totals = lax.psum(jnp.sum(jnp.exp(guided), 1), ('dp', 'tensor'))]
    reduce_scatter x2 -> x0, waiting for transfers between devices: 117 us -> none  [the longest x1 76.8 us: body(): lax.psum_scatter(jnp.concatenate([jnp.dot(all_rows, w_query, preferred_el...]
    pallas_call x0 -> x1, Pallas kernels: none -> 91 us  [body(): pl.pallas_call(kernel, out_shape=jax.ShapeDtypeStruct((128, 512), F32), i...]
    all_gather x3 -> x0, blocking collectives: 60.5 us -> none  [the longest x1 25.8 us: body(): normed_all = lax.all_gather(normed, 'tensor', axis=0, tiled=True)]
    all_gather x1 -> x0, waiting for transfers between devices: 53.8 us -> none  [body(): lax.all_gather(normed_all, 'dp', axis=1, tiled=True)]
    dot_general x7 -> x0, matrix products: 12.1 us -> none  [the longest x1 6.97 us: body(): jnp.dot(lax.all_gather(normed_all, 'dp', axis=1, tiled=True), w_head, pre...]
  transfers between devices with their start and end apart: 4 -> 0, of which waited for: 3 -> 0; matrix products, arithmetic and copies ran while one was open for 1% -> 0% of each run, Pallas kernels for 0% -> 0%
where the time goes in v1:
time: 94.1 us; the launch traced here: 93.9 us
  Pallas kernels  91 us (97%)
  local copies, waits for them, and re-layouts  2.93 us (3%)
    pallas_call x1, Pallas kernels, body(): pl.pallas_call(kernel, out_shape=jax.ShapeDtypeStruct((128, 512), F32), i...  91 us

profile of v1, /device:TPU:1, one launch (start us, length us, event | category | flops | bytes accessed | tf_op | source)
XLA Modules:
  0.0 93.9 jit_solution(3251140208709806529)
XLA Ops:
  0.0 1.3 %reshape.7.gain = bf16[1,512]{1,0:T(2,128)(2,1)} reshape(bf16[512]{0:T(512)(128)(2,1)} %param.20) | data formatting | bytes 2048 | tf_op jit(solution)/shard_map/reshape | solution.py:515
  1.3 91.0 %shard_map.109 = f32[128,512]{1,0:T(8,128)} custom-call(bf16[1,32,512]{2,1,0:T(8,128)(2,1)} %hidden.1, bf16[1,16,1,256,128]{4,3,2,1,0:T(8,128)(2,1)} %keys.1, bf16[1,16,1,256,128]{4,3,2,1,0:T(8,128)(2,1)} %vals.1, s32[1,16]{1,0:T(1,128)} %lens.1, s32[256,128]{1,0:T(8,128)} %ids.1, f32[2,128]{1,0:T(2,128)} %bitcast.1, bf16[512,1024]{1,0:T(8,128)(2,1)} %wq.1, ...), custom_call_target="tpu_custom_call" | custom-call | tf_op jit(solution)/shard_map/pallas_call | solution.py:447
  92.2 1.7 %copy.13 = f32[128,512]{1,0:T(8,128)} copy(f32[128,512]{1,0:T(8,128)} %shard_map.109) | data formatting | bytes 524288

commit v2 on v1

v2 whole, which is shorter than its diff:
```python
import jax
import jax.numpy as jnp
from jax import lax
from jax.experimental import pallas as pl
from jax.experimental.pallas import tpu as pltpu
from jax.sharding import PartitionSpec as P

MESH = pl.DeviceIdType.MESH
F32 = jnp.float32
BF16 = jnp.bfloat16
WIDTH = 8192
HEAD = 128
RING = 4
DP = 16
TEN = 8

rope_theta = 500000.0
penalty_step = 1.5
norm_eps = 1e-05


MARKS = False
open_scope = []


def mark(name):
    if MARKS:
        if open_scope:
            open_scope.pop().__exit__(None, None, None)
        if name:
            open_scope.append(jax.named_scope(name))
            open_scope[0].__enter__()


def routes():
    found = []
    for depth in range(5):
        for dx in range(RING):
            for dy in range(RING):
                if min(dx, RING - dx) + min(dy, RING - dy) != depth:
                    continue
                for quarter in range(4):
                    first, second = (dx, dy) if quarter < 2 else (dy, dx)
                    names = ("x", "y") if quarter < 2 else ("y", "x")
                    odd = quarter % 2
                    hops = []
                    if second == 0:
                        if first == 0:
                            hops += [(names[0], 1), (names[0], -1)]
                        elif first == 1 and not odd:
                            hops += [(names[0], 1)]
                        elif first == 3 and odd:
                            hops += [(names[0], -1)]
                        hops += [(names[1], 1), (names[1], -1)]
                    elif second == 1 and not odd:
                        hops += [(names[1], 1)]
                    elif second == 3 and odd:
                        hops += [(names[1], -1)]
                    found.append((depth, dx, dy, quarter, hops))
    return found


ROUTES = routes()
N_FORWARD = sum(len(r[4]) for r in ROUTES)
OFFSETS = [
    sorted({(r[1], r[2]) for r in ROUTES if r[0] == depth}) for depth in range(5)
]


def kernel(
    hidden,
    keys,
    vals,
    lens,
    ids,
    guid,
    wq,
    kvw,
    wo,
    gain,
    wh,
    out,
    h_c,
    wq_v,
    kvw_v,
    k_v,
    v_v,
    wo_v,
    wh_v,
    ids_v,
    gain_all,
    part,
    recv_b,
    q_s,
    att_s,
    att_b,
    att_all,
    part_d,
    recv_d,
    resid,
    buf,
    acc,
    ssq,
    counts,
    gcol,
    tot_one,
    tot_t,
    tot_two,
    tot_d,
    load_sem,
    w_recv,
    f_recv,
    sib_recv,
    one,
):
    S = lax.axis_index("stream")
    D = lax.axis_index("dp")
    T = lax.axis_index("tensor")
    zl, c = T // 2, T % 2
    x, y = D // RING, D % RING
    sib = (S, D, zl * 2 + 1 - c)
    names = ("w", "a", "gain", "b", "c", "d", "z", "f", "sib", "t", "s")
    send_of = {name: one.at[n] for n, name in enumerate(names)}
    recv_of = {name: one.at[len(names) + n] for n, name in enumerate(names)}

    def remote(src, dst, ssem, rsem, dev):
        copy = pltpu.make_async_remote_copy(
            src_ref=src,
            dst_ref=dst,
            send_sem=ssem,
            recv_sem=rsem,
            device_id=dev,
            device_id_type=MESH,
        )
        copy.start()

    def arrived(ref, rsem):
        pltpu.make_async_remote_copy(
            src_ref=ref,
            dst_ref=ref,
            send_sem=send_of["w"],
            recv_sem=rsem,
            device_id=sib,
            device_id_type=MESH,
        ).wait_recv()

    def left(ref, name):
        pltpu.make_async_remote_copy(
            src_ref=ref,
            dst_ref=ref,
            send_sem=send_of[name],
            recv_sem=recv_of[name],
            device_id=sib,
            device_id_type=MESH,
        ).wait_send()

    mark("p00_entry")
    barrier = pltpu.get_barrier_semaphore()
    for i in range(1, DP):
        pl.semaphore_signal(
            barrier, inc=1, device_id=(S, (D + i) % DP, T), device_id_type=MESH
        )
        pl.semaphore_signal(
            barrier, inc=1, device_id=(S, (D + i) % DP, zl * 2 + 1 - c), device_id_type=MESH
        )
    for i in range(1, 16):
        other = (S * TEN + T + i) % 16
        pl.semaphore_signal(
            barrier, inc=1, device_id=(other // TEN, D, other % TEN), device_id_type=MESH
        )

    loads = []

    def load(src, dst, sem=None):
        copy = pltpu.make_async_copy(src, dst, load_sem.at[len(loads)] if sem is None else sem)
        copy.start()
        loads.append(copy)
        return copy

    load(hidden.at[0], h_c.at[zl], recv_of["a"])
    l_wq = load(wq, wq_v.at[c])
    l_kv = load(kvw, kvw_v.at[c])
    l_ids = load(ids.at[pl.ds(S * 128, 128), :], ids_v)
    l_k = load(keys.at[0, :, 0], k_v)
    l_v = load(vals.at[0, :, 0], v_v)
    l_wo = load(wo, wo_v.at[c])
    pl.semaphore_wait(barrier, 45)

    mark("p01_hidden")
    for dz in (3, 2, 1):
        dev = (S, D, ((zl + dz) % 4) * 2 + c)
        remote(hidden.at[0], h_c.at[zl], send_of["a"], recv_of["a"], dev)
    remote(wq, wq_v.at[c], send_of["w"], w_recv.at[0], sib)
    remote(kvw, kvw_v.at[c], send_of["w"], w_recv.at[1], sib)
    gain_all[D] = gain[...].astype(F32).reshape(1, 512)
    l_wh = load(wh, wh_v)
    remote(wo, wo_v.at[c], send_of["w"], w_recv.at[2], sib)
    l_wq.wait()
    l_kv.wait()
    arrived(h_c, recv_of["a"])

    mark("p02_qkv")
    h = h_c[...].reshape(128, 512)
    for i in range(2):
        g = (c + i) % 2
        if i == 1:
            arrived(wq_v.at[g], w_recv.at[0])
            arrived(kvw_v.at[g], w_recv.at[1])
        for n in range(4):
            cols = pl.ds(n * 256, 256)
            r = jnp.dot(h, wq_v[g, :, cols], preferred_element_type=F32)
            part[:, g, :, cols] = r.reshape(8, 16, 256).astype(BF16)
        for n in range(2):
            cols = pl.ds(1024 + n * 128, 128)
            r = jnp.dot(h, kvw_v[g, :, n, :], preferred_element_type=F32)
            part[:, g, :, cols] = r.reshape(8, 16, 128).astype(BF16)
        for n in range(8):
            k = (D // 2 + 1 + n) % 8
            to = 4 * (k // 2) + 2 * c + k % 2
            if i == 1:
                remote(
                    part.at[k, g], recv_b.at[D], send_of["b"], recv_of["b"], (S, to, zl * 2 + g)
                )
                continue

            @pl.when(to == D)
            def _():
                pltpu.make_async_copy(part.at[k, g], recv_b.at[D], recv_of["b"]).start()

            @pl.when(to != D)
            def _():
                remote(
                    part.at[k, g], recv_b.at[D], send_of["b"], recv_of["b"], (S, to, zl * 2 + g)
                )
    for i in range(1, DP):
        to = (D + i) % DP
        remote(gain_all.at[D], gain_all.at[D], send_of["gain"], recv_of["gain"], (S, to, T))

    mark("p03_tables")
    lane = lax.broadcasted_iota(jnp.int32, (16, HEAD), 1)
    row = lax.broadcasted_iota(jnp.int32, (16, HEAD), 0)
    freq = jnp.exp(((lane % 64).astype(F32) * (2.0 / HEAD)) * (-jnp.log(F32(rope_theta))))
    position = jnp.zeros((16, HEAD), jnp.int32)
    for p in range(16):
        position = jnp.where(row == p, lens[0, p], position)
    angle = position.astype(F32) * freq
    cosine = jnp.cos(angle)
    sine = jnp.sin(angle) * jnp.where(lane < 64, -1.0, 1.0)

    l_ids.wait()
    base = (D * TEN + T) * 512
    ids_v[...] = jnp.transpose(ids_v[...]) - base
    for n in range(4):
        column = lax.broadcasted_iota(jnp.int32, (128, 128), 0) + n * 128

        def add(r, total):
            for k in range(8):
                here = ids_v[pl.ds(r * 8 + k, 1), :]
                total = total + jnp.where(column == here, 1.0, 0.0)
            return total

        total = lax.fori_loop(0, 16, add, jnp.zeros((128, 128), F32))
        counts[:, pl.ds(n * 128, 128)] = jnp.transpose(total) * penalty_step
    gcol[...] = jnp.transpose(jnp.broadcast_to(guid[pl.ds(S, 1), :], (128, 128)))

    mark("p04_sumwait")
    arrived(recv_b, recv_of["b"])
    qkv = recv_b[0].astype(F32)
    for i in range(1, DP):
        qkv = qkv + recv_b[i].astype(F32)

    mark("p05_rope")

    def turn(v):
        return v * cosine + pltpu.roll(v, 64, 1) * sine

    for g in range(8):
        q_s[:, g, :] = turn(qkv[:, g * HEAD : (g + 1) * HEAD])
    k_new = turn(qkv[:, 1024:1152]).astype(BF16).astype(F32)
    v_new = qkv[:, 1152:1280].astype(BF16).astype(F32)

    mark("p06_attn")
    l_k.wait()
    l_v.wait()
    scale = HEAD ** (-0.5)
    slot_at = lax.broadcasted_iota(jnp.int32, (8, 256), 1)
    for start in (0, 8):
        prompts = range(start, start + 8)
        q = [q_s[p].astype(BF16) for p in prompts]
        scores = [
            lax.dot_general(
                q[p - start], k_v[p], (((1,), (1,)), ((), ())), preferred_element_type=F32
            )
            for p in prompts
        ]
        k_own = jnp.concatenate([jnp.broadcast_to(k_new[p : p + 1], (8, HEAD)) for p in prompts])
        v_own = jnp.concatenate([jnp.broadcast_to(v_new[p : p + 1], (8, HEAD)) for p in prompts])
        q_all = jnp.concatenate([v.astype(F32) for v in q])
        e_own = jnp.exp(jnp.sum(q_all * k_own, axis=1, keepdims=True) * scale)
        e = jnp.concatenate(
            [
                jnp.where(slot_at < lens[0, p], jnp.exp(scores[p - start] * scale), 0.0)
                for p in prompts
            ]
        )
        den = jnp.sum(e, axis=1, keepdims=True) + e_own
        w = (e / den).astype(BF16)
        w_own = (e_own / den).astype(BF16).astype(F32)
        o = jnp.concatenate(
            [
                jnp.dot(
                    w[(p - start) * 8 : (p - start + 1) * 8],
                    v_v[p],
                    preferred_element_type=F32,
                )
                for p in prompts
            ]
        )
        att_s[pl.ds(start, 8)] = (o + w_own * v_own).reshape(8, 8, HEAD)
    for g in range(8):
        att_b[:, pl.ds(g * HEAD, HEAD)] = att_s[:, g, :].astype(BF16)

    mark("p07_gatherC")
    core = (D // 2) % 2
    slot = c * 8 + 2 * (D // 4) + D % 2
    for i in range(1, DP):
        to = (D + i) % DP
        remote(att_b, att_all.at[slot], send_of["c"], recv_of["c"], (S, to, zl * 2 + core))

    @pl.when(core == c)
    def _():
        pltpu.make_async_copy(att_b, att_all.at[slot], recv_of["c"]).start()

    @pl.when(core != c)
    def _():
        remote(att_b, att_all.at[slot], send_of["c"], recv_of["c"], sib)

    l_wo.wait()
    arrived(wo_v.at[1 - c], w_recv.at[2])
    arrived(att_all, recv_of["c"])

    mark("p08_outproj")
    a0 = att_all[pl.ds(0, 8)].reshape(128, 1024)
    a1 = att_all[pl.ds(8, 8)].reshape(128, 1024)
    for n in range(2):
        cols = pl.ds(n * 256, 256)
        r = jnp.dot(a0, wo_v[0, :, cols], preferred_element_type=F32)
        r = r + jnp.dot(a1, wo_v[1, :, cols], preferred_element_type=F32)
        part_d[:, :, cols] = r.reshape(4, 32, 256).astype(BF16)

    def owned(z):
        inner = ((z + 1) // 2) % 2
        half = inner * S + (1 - inner) * (1 - S)
        return half, 2 * half + inner * (z - 1) + (1 - inner) * (z // 3)

    for dz in (3, 2, 1):
        to = (zl + dz) % 4
        block = owned(to)[1]
        remote(
            part_d.at[block],
            recv_d.at[3 - dz],
            send_of["d"],
            recv_of["d"],
            (S, D, to * 2 + c),
        )
    mark("p09_sumwaitD")
    my_half, mine = owned(zl)
    my_j = 2 * (mine % 2) + c
    total = h_c[mine].astype(F32) + part_d[mine].astype(F32)
    arrived(recv_d, recv_of["d"])
    for i in range(3):
        total = total + recv_d[i].astype(F32)
    resid[...] = total.astype(BF16)

    mark("p10_z")
    place = buf.at[S, D, pl.ds(my_j * 32, 32), :]
    for z in range(4):
        at_home = jnp.logical_and(my_half == S, 2 * z + S == T)

        @pl.when(at_home)
        def _():
            pltpu.make_async_copy(resid, place, recv_of["z"]).start()

        @pl.when(jnp.logical_not(at_home))
        def _():
            remote(resid, place, send_of["z"], recv_of["z"], (my_half, D, 2 * z + S))

    arrived(gain_all.at[pl.ds(0, DP - 1)], recv_of["gain"])
    l_wh.wait()
    acc[...] = jnp.zeros_like(acc)
    ssq[...] = jnp.zeros_like(ssq)

    def neighbour(name, step):
        if name == "x":
            return (S, ((x + RING + step) % RING) * RING + y, T)
        return (S, x * RING + (y + RING + step) % RING, T)

    def slot_of(dx, dy):
        return ((x + RING - dx) % RING) * RING + (y + RING - dy) % RING

    def pass_on(dx, dy):
        slot = slot_of(dx, dy)
        later = []
        for _, _, _, quarter, hops in [r for r in ROUTES if r[1:3] == (dx, dy)]:
            piece = buf.at[c, slot, pl.ds(quarter * 32, 32), :]
            sem = f_recv.at[slot, quarter]
            if (dx, dy) != (0, 0):
                arrived(piece, sem)
            else:
                later += [(piece, sem, hop) for hop in hops[2:]]
                hops = hops[:2]
            for hop in hops:
                remote(piece, piece, send_of["f"], sem, neighbour(*hop))
        for piece, sem, hop in later:
            remote(piece, piece, send_of["f"], sem, neighbour(*hop))
        whole = buf.at[c, slot]
        remote(whole, whole, send_of["sib"], sib_recv.at[slot], sib)

    def head(dx, dy):
        slot = slot_of(dx, dy)
        arrived(buf.at[1 - c, slot], sib_recv.at[slot])
        v = buf[:, slot].reshape(256, 512).astype(F32)
        v2 = v * v
        ssq[...] += v2[:, 0:128] + v2[:, 128:256] + v2[:, 256:384] + v2[:, 384:512]
        w = (v * gain_all[slot]).astype(BF16)
        acc[...] += jnp.dot(
            w,
            wh_v[pl.ds(pl.multiple_of(slot * 512, 512), 512), :],
            preferred_element_type=F32,
        )

    mark("p10b_zwait")
    arrived(buf.at[c, D], recv_of["z"])
    order = [offset for level in OFFSETS for offset in level]
    for n, offset in enumerate(order):
        mark(f"p11_gatherF{n:02d}")
        pass_on(*offset)
        if n >= 2:
            mark(f"p12_head{n-2:02d}")
            head(*order[n - 2])
    mark("p13_head14")
    head(*order[14])
    mark("p13_head15")
    head(*order[15])

    mark("p16_guided")
    inv = lax.rsqrt(jnp.sum(ssq[...], axis=1, keepdims=True) / WIDTH + norm_eps)
    cond = acc[0:128, :] * inv[0:128]
    uncond = acc[128:256, :] * inv[128:256]
    guide = gcol[:, 0:1]
    guided = uncond + guide * (cond - uncond) - counts[...]
    acc[0:128, :] = guided
    e = jnp.exp(guided)
    e = e[:, 0:128] + e[:, 128:256] + e[:, 256:384] + e[:, 384:512]
    mark("p17_total_t")
    tot_one[...] = jnp.sum(jnp.transpose(e), axis=0, keepdims=True)
    for i in range(1, TEN):
        to = (T + i) % TEN
        remote(tot_one, tot_t.at[i - 1], send_of["t"], recv_of["t"], (S, D, to))
    arrived(tot_t, recv_of["t"])
    mark("p18_total_d")
    tot_two[...] = tot_one[...] + jnp.sum(tot_t[...], axis=0)
    for i in range(1, DP):
        to = (D + i) % DP
        remote(tot_two, tot_d.at[i - 1], send_of["s"], recv_of["s"], (S, to, T))
    arrived(tot_d, recv_of["s"])
    totals = tot_two[...] + jnp.sum(tot_d[...], axis=0)
    log_total = jnp.transpose(jnp.broadcast_to(jnp.log(totals), (128, 128)))
    for n in range(4):
        cols = pl.ds(n * 128, 128)
        out[:, cols] = acc[0:128, cols] - log_total

    mark("p19_waitsend")
    left(wq_v.at[0], "w")
    left(kvw_v.at[0], "w")
    left(wo_v.at[0], "w")
    left(h_c.at[pl.ds(0, 3)], "a")
    left(gain_all.at[pl.ds(0, DP - 1)], "gain")
    left(part_d.at[pl.ds(0, 3)], "d")
    left(buf.at[0, pl.ds(0, 15)], "f")
    left(buf.at[0], "sib")
    left(tot_t, "t")
    left(tot_d, "s")
    kept_c = core == c
    kept_z = jnp.logical_and(my_half == S, c == S)

    @pl.when(kept_c)
    def _():
        left(recv_b.at[pl.ds(0, DP - 1)], "b")
        left(att_all.at[pl.ds(0, DP - 1)], "c")

    @pl.when(jnp.logical_not(kept_c))
    def _():
        left(recv_b, "b")
        left(att_all, "c")

    @pl.when(kept_z)
    def _():
        left(part_d.at[pl.ds(0, 3)], "z")

    @pl.when(jnp.logical_not(kept_z))
    def _():
        left(part_d, "z")

    mark(None)


def body(hidden, keys, vals, lens, ids, guid, wq, kvw, wo, gain, wh):
    dma = pltpu.SemaphoreType.DMA
    anywhere = pl.BlockSpec(memory_space=pl.ANY)
    vmem = pl.BlockSpec(memory_space=pltpu.VMEM)
    smem = pl.BlockSpec(memory_space=pltpu.SMEM)
    return pl.pallas_call(
        kernel,
        out_shape=jax.ShapeDtypeStruct((128, 512), F32),
        in_specs=[
            anywhere,
            anywhere,
            anywhere,
            smem,
            anywhere,
            vmem,
            anywhere,
            anywhere,
            anywhere,
            vmem,
            anywhere,
        ],
        out_specs=vmem,
        scratch_shapes=[
            pltpu.VMEM((4, 32, 512), BF16),
            pltpu.VMEM((2, 512, 1024), BF16),
            pltpu.VMEM((2, 512, 2, 128), BF16),
            pltpu.VMEM((16, 256, 128), BF16),
            pltpu.VMEM((16, 256, 128), BF16),
            pltpu.VMEM((2, 1024, 512), BF16),
            pltpu.VMEM((8192, 512), BF16),
            pltpu.VMEM((128, 128), jnp.int32),
            pltpu.VMEM((DP, 1, 512), F32),
            pltpu.VMEM((8, 2, 16, 1280), BF16),
            pltpu.VMEM((DP, 16, 1280), BF16),
            pltpu.VMEM((16, 8, 128), F32),
            pltpu.VMEM((16, 8, 128), F32),
            pltpu.VMEM((16, 1024), BF16),
            pltpu.VMEM((DP, 16, 1024), BF16),
            pltpu.VMEM((4, 32, 512), BF16),
            pltpu.VMEM((3, 32, 512), BF16),
            pltpu.VMEM((32, 512), BF16),
            pltpu.VMEM((2, DP, 128, 512), BF16),
            pltpu.VMEM((256, 512), F32),
            pltpu.VMEM((256, 128), F32),
            pltpu.VMEM((128, 512), F32),
            pltpu.VMEM((128, 128), F32),
            pltpu.VMEM((1, 128), F32),
            pltpu.VMEM((TEN - 1, 1, 128), F32),
            pltpu.VMEM((1, 128), F32),
            pltpu.VMEM((DP - 1, 1, 128), F32),
            dma((9,)),
            dma((3,)),
            dma((DP, 4)),
            dma((DP,)),
            dma((22,)),
        ],
        compiler_params=pltpu.CompilerParams(
            collective_id=0, has_side_effects=True, vmem_limit_bytes=60 * 1024 * 1024
        ),
    )(hidden, keys, vals, lens, ids, guid.reshape(2, 128), wq, kvw, wo, gain, wh)


def solution(mesh):
    return jax.shard_map(
        body,
        mesh=mesh,
        in_specs=(
            P("stream", "tensor", "dp"),
            P("stream", "dp", "tensor", None, None),
            P("stream", "dp", "tensor", None, None),
            P("stream", "dp"),
            P(),
            P(),
            P("dp", "tensor"),
            P("dp", None, "tensor"),
            P("tensor", "dp"),
            P("dp"),
            P(None, ("dp", "tensor")),
        ),
        out_specs=P("stream", ("dp", "tensor")),
        check_vma=False,
    )
```

time: 94.1 us -> 81.2 us (0.86)
  Pallas kernels: 91 us -> 79.4 us
  local copies, waits for them, and re-layouts: 2.93 us -> 1.67 us
    pallas_call x1, Pallas kernels: 91 us -> 79.4 us  [body(): pl.pallas_call(kernel, out_shape=jax.ShapeDtypeStruct((128, 512), F32), i...]
    reshape x1 -> x0, local copies, waits for them, and re-layouts: 1.26 us -> none  [body(): gain.reshape(1, 512)]
where the time goes in v2:
time: 81.2 us; the launch traced here: 81 us
  Pallas kernels  79.4 us (98%)
  local copies, waits for them, and re-layouts  1.67 us (2%)
    pallas_call x1, Pallas kernels, body(): pl.pallas_call(kernel, out_shape=jax.ShapeDtypeStruct((128, 512), F32), i...  79.4 us
    unnamed x1, local copies, waits for them, and re-layouts  1.67 us

profile of v2, /device:TPU:1, one launch (start us, length us, event | category | flops | bytes accessed | tf_op | source)
XLA Modules:
  0.0 81.0 jit_solution(15087704396605628529)
XLA Ops:
  0.0 79.4 %shard_map.109 = f32[128,512]{1,0:T(8,128)} custom-call(bf16[1,32,512]{2,1,0:T(8,128)(2,1)} %hidden.1, bf16[1,16,1,256,128]{4,3,2,1,0:T(8,128)(2,1)} %keys.1, bf16[1,16,1,256,128]{4,3,2,1,0:T(8,128)(2,1)} %vals.1, s32[1,16]{1,0:T(1,128)} %lens.1, s32[256,128]{1,0:T(8,128)} %ids.1, f32[2,128]{1,0:T(2,128)} %bitcast.1, bf16[512,1024]{1,0:T(8,128)(2,1)} %wq.1, ...), custom_call_target="tpu_custom_call" | custom-call | tf_op jit(solution)/shard_map/pallas_call | solution.py:513
  79.4 1.7 %copy.13 = f32[128,512]{1,0:T(8,128)} copy(f32[128,512]{1,0:T(8,128)} %shard_map.109) | data formatting | bytes 524288

commit v3 on v2

--- a/solution.py
+++ b/solution.py
@@ -1,3 +1,5 @@
+import heapq
+
 import jax
 import jax.numpy as jnp
 from jax import lax
@@ -60,11 +62,50 @@
     return found
 
 
-ROUTES = routes()
-N_FORWARD = sum(len(r[4]) for r in ROUTES)
-OFFSETS = [
-    sorted({(r[1], r[2]) for r in ROUTES if r[0] == depth}) for depth in range(5)
-]
+HOPS = {r[1:4]: r[4] for r in routes()}
+N_FORWARD = sum(len(hops) for hops in HOPS.values())
+PLACE = [4 * (g // 4) + 2 * (g % 2) + (g // 2) % 2 for g in range(8)]
+
+
+def onward(piece, hop):
+    dx, dy, quarter = piece
+    axis, step = hop
+    if axis == "x":
+        return (dx + step) % RING, dy, quarter
+    return dx, (dy + step) % RING, quarter
+
+
+def further(piece):
+    return max([1 + further(onward(piece, hop)) for hop in HOPS[piece]], default=0)
+
+
+def forwards(piece):
+    return sorted(HOPS[piece], key=lambda hop: -further(onward(piece, hop)))
+
+
+def plan():
+    free, arrivals, order = {}, [], []
+
+    def send(piece, hop, now):
+        free[hop] = max(free.get(hop, 0.0), now) + 0.7
+        heapq.heappush(arrivals, (free[hop] + 1.66, len(order), onward(piece, hop)))
+
+    own = [(0, 0, quarter) for quarter in range(4)]
+    first = [(piece, hop) for piece in own for hop in HOPS[piece][:2]]
+    first += [(piece, hop) for piece in own for hop in HOPS[piece][2:]]
+    for piece, hop in first:
+        send(piece, hop, 0.0)
+    now = 0.0
+    while arrivals:
+        when, _, piece = heapq.heappop(arrivals)
+        now = max(now, when) + 0.02
+        order.append(piece)
+        for hop in forwards(piece):
+            send(piece, hop, now)
+    return order
+
+
+ORDER = plan()
 
 
 def kernel(
@@ -104,11 +145,10 @@
     counts,
     gcol,
     tot_one,
-    tot_t,
-    tot_two,
-    tot_d,
+    tot_all,
     load_sem,
     w_recv,
+    z_recv,
     f_recv,
     sib_recv,
     one,
@@ -119,7 +159,7 @@
     zl, c = T // 2, T % 2
     x, y = D // RING, D % RING
     sib = (S, D, zl * 2 + 1 - c)
-    names = ("w", "a", "gain", "b", "c", "d", "z", "f", "sib", "t", "s")
+    names = ("w", "a", "gain", "b", "c", "d", "z", "f", "sib", "t")
     send_of = {name: one.at[n] for n, name in enumerate(names)}
     recv_of = {name: one.at[len(names) + n] for n, name in enumerate(names)}
 
@@ -172,15 +212,22 @@
     loads = []
 
     def load(src, dst, sem=None):
-        copy = pltpu.make_async_copy(src, dst, load_sem.at[len(loads)] if sem is None else sem)
+        if sem is None:
+            sem = load_sem.at[len(loads)]
+            loads.append(sem)
+        copy = pltpu.make_async_copy(src, dst, sem)
         copy.start()
-        loads.append(copy)
         return copy
 
-    load(hidden.at[0], h_c.at[zl], recv_of["a"])
+    load(hidden.at[0, pl.ds(c * 16, 16)], h_c.at[T], recv_of["a"])
     l_wq = load(wq, wq_v.at[c])
     l_kv = load(kvw, kvw_v.at[c])
-    l_ids = load(ids.at[pl.ds(S * 128, 128), :], ids_v)
+    for g in range(8):
+        load(
+            ids.at[pl.ds(S * 128 + PLACE[g] * 16, 16), :],
+            ids_v.at[pl.ds(g * 16, 16), :],
+            load_sem.at[8],
+        )
     l_k = load(keys.at[0, :, 0], k_v)
     l_v = load(vals.at[0, :, 0], v_v)
     l_wo = load(wo, wo_v.at[c])
@@ -188,8 +235,12 @@
 
     mark("p01_hidden")
     for dz in (3, 2, 1):
-        dev = (S, D, ((zl + dz) % 4) * 2 + c)
-        remote(hidden.at[0], h_c.at[zl], send_of["a"], recv_of["a"], dev)
+        for core in (0, 1):
+            dev = (S, D, ((zl + dz) % 4) * 2 + core)
+            remote(
+                hidden.at[0, pl.ds(core * 16, 16)], h_c.at[T], send_of["a"], recv_of["a"], dev
+            )
+    remote(hidden.at[0, pl.ds(16 - c * 16, 16)], h_c.at[T], send_of["a"], recv_of["a"], sib)
     remote(wq, wq_v.at[c], send_of["w"], w_recv.at[0], sib)
     remote(kvw, kvw_v.at[c], send_of["w"], w_recv.at[1], sib)
     gain_all[D] = gain[...].astype(F32).reshape(1, 512)
@@ -216,7 +267,7 @@
             part[:, g, :, cols] = r.reshape(8, 16, 128).astype(BF16)
         for n in range(8):
             k = (D // 2 + 1 + n) % 8
-            to = 4 * (k // 2) + 2 * c + k % 2
+            to = 2 * k + c
             if i == 1:
                 remote(
                     part.at[k, g], recv_b.at[D], send_of["b"], recv_of["b"], (S, to, zl * 2 + g)
@@ -247,7 +298,7 @@
     cosine = jnp.cos(angle)
     sine = jnp.sin(angle) * jnp.where(lane < 64, -1.0, 1.0)
 
-    l_ids.wait()
+    pltpu.make_async_copy(ids.at[pl.ds(0, 128), :], ids_v, load_sem.at[8]).wait()
     base = (D * TEN + T) * 512
     ids_v[...] = jnp.transpose(ids_v[...]) - base
     for n in range(4):
@@ -261,7 +312,9 @@
 
         total = lax.fori_loop(0, 16, add, jnp.zeros((128, 128), F32))
         counts[:, pl.ds(n * 128, 128)] = jnp.transpose(total) * penalty_step
-    gcol[...] = jnp.transpose(jnp.broadcast_to(guid[pl.ds(S, 1), :], (128, 128)))
+    guide = jnp.transpose(jnp.broadcast_to(guid[pl.ds(S, 1), :], (128, 128)))
+    for g in range(8):
+        gcol[g * 16 : (g + 1) * 16] = guide[PLACE[g] * 16 : (PLACE[g] + 1) * 16]
 
     mark("p04_sumwait")
     arrived(recv_b, recv_of["b"])
@@ -321,8 +374,8 @@
         att_b[:, pl.ds(g * HEAD, HEAD)] = att_s[:, g, :].astype(BF16)
 
     mark("p07_gatherC")
-    core = (D // 2) % 2
-    slot = c * 8 + 2 * (D // 4) + D % 2
+    core = D % 2
+    slot = c * 8 + D // 2
     for i in range(1, DP):
         to = (D + i) % DP
         remote(att_b, att_all.at[slot], send_of["c"], recv_of["c"], (S, to, zl * 2 + core))
@@ -366,7 +419,7 @@
     mark("p09_sumwaitD")
     my_half, mine = owned(zl)
     my_j = 2 * (mine % 2) + c
-    total = h_c[mine].astype(F32) + part_d[mine].astype(F32)
+    total = h_c[pl.ds(2 * mine, 2)].reshape(32, 512).astype(F32) + part_d[mine].astype(F32)
     arrived(recv_d, recv_of["d"])
     for i in range(3):
         total = total + recv_d[i].astype(F32)
@@ -379,11 +432,11 @@
 
         @pl.when(at_home)
         def _():
-            pltpu.make_async_copy(resid, place, recv_of["z"]).start()
+            pltpu.make_async_copy(resid, place, z_recv.at[my_j]).start()
 
         @pl.when(jnp.logical_not(at_home))
         def _():
-            remote(resid, place, send_of["z"], recv_of["z"], (my_half, D, 2 * z + S))
+            remote(resid, place, send_of["z"], z_recv.at[my_j], (my_half, D, 2 * z + S))
 
     arrived(gain_all.at[pl.ds(0, DP - 1)], recv_of["gain"])
     l_wh.wait()
@@ -398,23 +451,15 @@
     def slot_of(dx, dy):
         return ((x + RING - dx) % RING) * RING + (y + RING - dy) % RING
 
-    def pass_on(dx, dy):
-        slot = slot_of(dx, dy)
-        later = []
-        for _, _, _, quarter, hops in [r for r in ROUTES if r[1:3] == (dx, dy)]:
-            piece = buf.at[c, slot, pl.ds(quarter * 32, 32), :]
-            sem = f_recv.at[slot, quarter]
-            if (dx, dy) != (0, 0):
-                arrived(piece, sem)
-            else:
-                later += [(piece, sem, hop) for hop in hops[2:]]
-                hops = hops[:2]
-            for hop in hops:
-                remote(piece, piece, send_of["f"], sem, neighbour(*hop))
-        for piece, sem, hop in later:
-            remote(piece, piece, send_of["f"], sem, neighbour(*hop))
-        whole = buf.at[c, slot]
-        remote(whole, whole, send_of["sib"], sib_recv.at[slot], sib)
+    def send_on(piece, hops):
+        slot, quarter = slot_of(*piece[:2]), piece[2]
+        rows = buf.at[c, slot, pl.ds(quarter * 32, 32), :]
+        for hop in hops:
+            remote(rows, rows, send_of["f"], f_recv.at[slot, quarter], neighbour(*hop))
+
+    def share(dx, dy):
+        whole = buf.at[c, slot_of(dx, dy)]
+        remote(whole, whole, send_of["sib"], sib_recv.at[slot_of(dx, dy)], sib)
 
     def head(dx, dy):
         slot = slot_of(dx, dy)
@@ -430,18 +475,31 @@
         )
 
     mark("p10b_zwait")
-    arrived(buf.at[c, D], recv_of["z"])
-    order = [offset for level in OFFSETS for offset in level]
-    for n, offset in enumerate(order):
-        mark(f"p11_gatherF{n:02d}")
-        pass_on(*offset)
-        if n >= 2:
-            mark(f"p12_head{n-2:02d}")
-            head(*order[n - 2])
-    mark("p13_head14")
-    head(*order[14])
-    mark("p13_head15")
-    head(*order[15])
+    for quarter in range(4):
+        arrived(buf.at[c, D, pl.ds(quarter * 32, 32), :], z_recv.at[quarter])
+        send_on((0, 0, quarter), HOPS[(0, 0, quarter)][:2])
+    mark("p11_own")
+    for quarter in range(4):
+        send_on((0, 0, quarter), HOPS[(0, 0, quarter)][2:])
+    share(0, 0)
+    complete = [(0, (0, 0))]
+    held = {}
+    for n, piece in enumerate(ORDER):
+        if n % 10 == 0:
+            mark(f"p12_pieces{n:02d}")
+        dx, dy, quarter = piece
+        slot = slot_of(dx, dy)
+        arrived(buf.at[c, slot, pl.ds(quarter * 32, 32), :], f_recv.at[slot, quarter])
+        send_on(piece, forwards(piece))
+        held[dx, dy] = held.get((dx, dy), 0) + 1
+        if held[dx, dy] == 4:
+            share(dx, dy)
+            complete.append((n, (dx, dy)))
+        if complete and n - complete[0][0] >= 8:
+            head(*complete.pop(0)[1])
+    mark("p13_lastheads")
+    for _, offset in complete:
+        head(*offset)
 
     mark("p16_guided")
     inv = lax.rsqrt(jnp.sum(ssq[...], axis=1, keepdims=True) / WIDTH + norm_eps)
@@ -452,35 +510,38 @@
     acc[0:128, :] = guided
     e = jnp.exp(guided)
     e = e[:, 0:128] + e[:, 128:256] + e[:, 256:384] + e[:, 384:512]
-    mark("p17_total_t")
+    mark("p17_total")
     tot_one[...] = jnp.sum(jnp.transpose(e), axis=0, keepdims=True)
-    for i in range(1, TEN):
-        to = (T + i) % TEN
-        remote(tot_one, tot_t.at[i - 1], send_of["t"], recv_of["t"], (S, D, to))
-    arrived(tot_t, recv_of["t"])
-    mark("p18_total_d")
-    tot_two[...] = tot_one[...] + jnp.sum(tot_t[...], axis=0)
-    for i in range(1, DP):
-        to = (D + i) % DP
-        remote(tot_two, tot_d.at[i - 1], send_of["s"], recv_of["s"], (S, to, T))
-    arrived(tot_d, recv_of["s"])
-    totals = tot_two[...] + jnp.sum(tot_d[...], axis=0)
+
+    def tell(i, carry):
+        to = (D * TEN + T + i) % (DP * TEN)
+        remote(
+            tot_one, tot_all.at[i - 1], send_of["t"], recv_of["t"], (S, to // TEN, to % TEN)
+        )
+        return carry
+
+    lax.fori_loop(1, DP * TEN, tell, 0)
+    arrived(tot_all, recv_of["t"])
+    mark("p18_out")
+    totals = tot_one[...] + jnp.sum(tot_all[...], axis=0)
     log_total = jnp.transpose(jnp.broadcast_to(jnp.log(totals), (128, 128)))
-    for n in range(4):
-        cols = pl.ds(n * 128, 128)
-        out[:, cols] = acc[0:128, cols] - log_total
+    for g in range(8):
+        for n in range(4):
+            cols = pl.ds(n * 128, 128)
+            out[pl.ds(PLACE[g] * 16, 16), cols] = (
+                acc[pl.ds(g * 16, 16), cols] - log_total[g * 16 : (g + 1) * 16]
+            )
 
     mark("p19_waitsend")
     left(wq_v.at[0], "w")
     left(kvw_v.at[0], "w")
     left(wo_v.at[0], "w")
-    left(h_c.at[pl.ds(0, 3)], "a")
+    left(h_c.at[pl.ds(0, 7)], "a")
     left(gain_all.at[pl.ds(0, DP - 1)], "gain")
     left(part_d.at[pl.ds(0, 3)], "d")
     left(buf.at[0, pl.ds(0, 15)], "f")
     left(buf.at[0], "sib")
-    left(tot_t, "t")
-    left(tot_d, "s")
+    left(tot_all, "t")
     kept_c = core == c
     kept_z = jnp.logical_and(my_half == S, c == S)
 
@@ -528,7 +589,7 @@
         ],
         out_specs=vmem,
         scratch_shapes=[
-            pltpu.VMEM((4, 32, 512), BF16),
+            pltpu.VMEM((TEN, 16, 512), BF16),
             pltpu.VMEM((2, 512, 1024), BF16),
             pltpu.VMEM((2, 512, 2, 128), BF16),
             pltpu.VMEM((16, 256, 128), BF16),
@@ -552,14 +613,13 @@
             pltpu.VMEM((128, 512), F32),
             pltpu.VMEM((128, 128), F32),
             pltpu.VMEM((1, 128), F32),
-            pltpu.VMEM((TEN - 1, 1, 128), F32),
-            pltpu.VMEM((1, 128), F32),
-            pltpu.VMEM((DP - 1, 1, 128), F32),
+            pltpu.VMEM((DP * TEN - 1, 1, 128), F32),
             dma((9,)),
             dma((3,)),
+            dma((4,)),
             dma((DP, 4)),
             dma((DP,)),
-            dma((22,)),
+            dma((20,)),
         ],
         compiler_params=pltpu.CompilerParams(
             collective_id=0, has_side_effects=True, vmem_limit_bytes=60 * 1024 * 1024

time: 81.2 us -> 73.9 us (0.910)
  Pallas kernels: 79.4 us -> 72.1 us
    pallas_call x1, Pallas kernels: 79.4 us -> 72.1 us  [body(): pl.pallas_call(kernel, out_shape=jax.ShapeDtypeStruct((128, 512), F32), i...]
where the time goes in v3:
time: 73.9 us; the launch traced here: 73.8 us
  Pallas kernels  72.1 us (98%)
  local copies, waits for them, and re-layouts  1.67 us (2%)
    pallas_call x1, Pallas kernels, body(): pl.pallas_call(kernel, out_shape=jax.ShapeDtypeStruct((128, 512), F32), i...  72.1 us
    unnamed x1, local copies, waits for them, and re-layouts  1.67 us

profile of v3, /device:TPU:1, one launch (start us, length us, event | category | flops | bytes accessed | tf_op | source)
XLA Modules:
  0.0 73.8 jit_solution(7927762736182179021)
XLA Ops:
  0.0 72.1 %shard_map.109 = f32[128,512]{1,0:T(8,128)} custom-call(bf16[1,32,512]{2,1,0:T(8,128)(2,1)} %hidden.1, bf16[1,16,1,256,128]{4,3,2,1,0:T(8,128)(2,1)} %keys.1, bf16[1,16,1,256,128]{4,3,2,1,0:T(8,128)(2,1)} %vals.1, s32[1,16]{1,0:T(1,128)} %lens.1, s32[256,128]{1,0:T(8,128)} %ids.1, f32[2,128]{1,0:T(2,128)} %bitcast.1, bf16[512,1024]{1,0:T(8,128)(2,1)} %wq.1, ...), custom_call_target="tpu_custom_call" | custom-call | tf_op jit(solution)/shard_map/pallas_call | solution.py:574
  72.1 1.7 %copy.13 = f32[128,512]{1,0:T(8,128)} copy(f32[128,512]{1,0:T(8,128)} %shard_map.109) | data formatting | bytes 524288

commit v4 on v3

--- a/solution.py
+++ b/solution.py
@@ -106,6 +106,11 @@
 
 
 ORDER = plan()
+FAR = (2, 1, 3, 0)
+PLANE = sorted(
+    [(dx, dy) for dx in range(RING) for dy in range(RING)],
+    key=lambda o: -min(o[0], RING - o[0]) - min(o[1], RING - o[1]),
+)
 
 
 def kernel(
@@ -124,6 +129,7 @@
     h_c,
     wq_v,
     kvw_v,
+    kv_v,
     k_v,
     v_v,
     wo_v,
@@ -149,6 +155,7 @@
     load_sem,
     w_recv,
     z_recv,
+    c_recv,
     f_recv,
     sib_recv,
     one,
@@ -194,6 +201,9 @@
             device_id_type=MESH,
         ).wait_send()
 
+    def peer(dx, dy):
+        return ((x + dx) % RING) * RING + (y + dy) % RING
+
     mark("p00_entry")
     barrier = pltpu.get_barrier_semaphore()
     for i in range(1, DP):
@@ -221,7 +231,7 @@
 
     load(hidden.at[0, pl.ds(c * 16, 16)], h_c.at[T], recv_of["a"])
     l_wq = load(wq, wq_v.at[c])
-    l_kv = load(kvw, kvw_v.at[c])
+    l_kv = load(kvw, kvw_v)
     for g in range(8):
         load(
             ids.at[pl.ds(S * 128 + PLACE[g] * 16, 16), :],
@@ -242,12 +252,14 @@
             )
     remote(hidden.at[0, pl.ds(16 - c * 16, 16)], h_c.at[T], send_of["a"], recv_of["a"], sib)
     remote(wq, wq_v.at[c], send_of["w"], w_recv.at[0], sib)
-    remote(kvw, kvw_v.at[c], send_of["w"], w_recv.at[1], sib)
     gain_all[D] = gain[...].astype(F32).reshape(1, 512)
     l_wh = load(wh, wh_v)
     remote(wo, wo_v.at[c], send_of["w"], w_recv.at[2], sib)
+    l_kv.wait()
+    for n in range(2):
+        kv_v[c, :, n * 128 : (n + 1) * 128] = kvw_v[:, n, :]
     l_wq.wait()
-    l_kv.wait()
+    remote(kv_v.at[c], kv_v.at[c], send_of["w"], w_recv.at[1], sib)
     arrived(h_c, recv_of["a"])
 
     mark("p02_qkv")
@@ -256,18 +268,16 @@
         g = (c + i) % 2
         if i == 1:
             arrived(wq_v.at[g], w_recv.at[0])
-            arrived(kvw_v.at[g], w_recv.at[1])
+            arrived(kv_v.at[g], w_recv.at[1])
         for n in range(4):
             cols = pl.ds(n * 256, 256)
             r = jnp.dot(h, wq_v[g, :, cols], preferred_element_type=F32)
             part[:, g, :, cols] = r.reshape(8, 16, 256).astype(BF16)
-        for n in range(2):
-            cols = pl.ds(1024 + n * 128, 128)
-            r = jnp.dot(h, kvw_v[g, :, n, :], preferred_element_type=F32)
-            part[:, g, :, cols] = r.reshape(8, 16, 128).astype(BF16)
+        r = jnp.dot(h, kv_v[g], preferred_element_type=F32)
+        part[:, g, :, pl.ds(1024, 256)] = r.reshape(8, 16, 256).astype(BF16)
         for n in range(8):
-            k = (D // 2 + 1 + n) % 8
-            to = 2 * k + c
+            to = peer(FAR[n // 2], (y + c) % 2 + 2 - 2 * (n % 2))
+            k = to // 2
             if i == 1:
                 remote(
                     part.at[k, g], recv_b.at[D], send_of["b"], recv_of["b"], (S, to, zl * 2 + g)
@@ -376,46 +386,55 @@
     mark("p07_gatherC")
     core = D % 2
     slot = c * 8 + D // 2
-    for i in range(1, DP):
-        to = (D + i) % DP
-        remote(att_b, att_all.at[slot], send_of["c"], recv_of["c"], (S, to, zl * 2 + core))
+    for dx, dy in PLANE:
+        if (dx, dy) != (0, 0):
+            to = peer(dx, dy)
+            remote(att_b, att_all.at[slot], send_of["c"], c_recv.at[x], (S, to, zl * 2 + core))
 
     @pl.when(core == c)
     def _():
-        pltpu.make_async_copy(att_b, att_all.at[slot], recv_of["c"]).start()
+        pltpu.make_async_copy(att_b, att_all.at[slot], c_recv.at[x]).start()
 
     @pl.when(core != c)
     def _():
-        remote(att_b, att_all.at[slot], send_of["c"], recv_of["c"], sib)
+        remote(att_b, att_all.at[slot], send_of["c"], c_recv.at[x], sib)
 
     l_wo.wait()
     arrived(wo_v.at[1 - c], w_recv.at[2])
-    arrived(att_all, recv_of["c"])
-
-    mark("p08_outproj")
-    a0 = att_all[pl.ds(0, 8)].reshape(128, 1024)
-    a1 = att_all[pl.ds(8, 8)].reshape(128, 1024)
-    for n in range(2):
-        cols = pl.ds(n * 256, 256)
-        r = jnp.dot(a0, wo_v[0, :, cols], preferred_element_type=F32)
-        r = r + jnp.dot(a1, wo_v[1, :, cols], preferred_element_type=F32)
-        part_d[:, :, cols] = r.reshape(4, 32, 256).astype(BF16)
+
+    for pair in ((2, 1), (3, 0)):
+        blocks = [(x + dx) % RING for dx in pair]
+        for block in blocks:
+            arrived(att_all.at[pl.ds(0, 4)], c_recv.at[block])
+        mark(f"p08_outproj{pair[0]}")
+        a0 = jnp.concatenate([att_all[pl.ds(2 * b, 2)].reshape(32, 1024) for b in blocks])
+        a1 = jnp.concatenate([att_all[pl.ds(8 + 2 * b, 2)].reshape(32, 1024) for b in blocks])
+        for n in range(2):
+            cols = pl.ds(n * 256, 256)
+            r = jnp.dot(a0, wo_v[0, :, cols], preferred_element_type=F32)
+            r = r + jnp.dot(a1, wo_v[1, :, cols], preferred_element_type=F32)
+            for m, block in enumerate(blocks):
+                part_d[block, :, cols] = r[m * 32 : (m + 1) * 32].astype(BF16)
+        for block in blocks:
+            other = (block // 2 - S) * (block // 2 - S)
+            to = (1 - other) * (1 + block % 2) + other * 3 * (block % 2)
+
+            @pl.when(to != zl)
+            def _():
+                remote(
+                    part_d.at[block],
+                    recv_d.at[(zl - to + 3) % 4],
+                    send_of["d"],
+                    recv_of["d"],
+                    (S, D, to * 2 + c),
+                )
+        mark(f"p08b_wait{pair[0]}")
 
     def owned(z):
         inner = ((z + 1) // 2) % 2
         half = inner * S + (1 - inner) * (1 - S)
         return half, 2 * half + inner * (z - 1) + (1 - inner) * (z // 3)
 
-    for dz in (3, 2, 1):
-        to = (zl + dz) % 4
-        block = owned(to)[1]
-        remote(
-            part_d.at[block],
-            recv_d.at[3 - dz],
-            send_of["d"],
-            recv_of["d"],
-            (S, D, to * 2 + c),
-        )
     mark("p09_sumwaitD")
     my_half, mine = owned(zl)
     my_j = 2 * (mine % 2) + c
@@ -513,14 +532,11 @@
     mark("p17_total")
     tot_one[...] = jnp.sum(jnp.transpose(e), axis=0, keepdims=True)
 
-    def tell(i, carry):
-        to = (D * TEN + T + i) % (DP * TEN)
-        remote(
-            tot_one, tot_all.at[i - 1], send_of["t"], recv_of["t"], (S, to // TEN, to % TEN)
-        )
-        return carry
-
-    lax.fori_loop(1, DP * TEN, tell, 0)
+    for n, (dx, dy) in enumerate(PLANE):
+        for dt in range(TEN):
+            if (dx, dy, dt) != (0, 0, 0):
+                to = (S, peer(dx, dy), (T + dt) % TEN)
+                remote(tot_one, tot_all.at[n * TEN + dt - n // 15], send_of["t"], recv_of["t"], to)
     arrived(tot_all, recv_of["t"])
     mark("p18_out")
     totals = tot_one[...] + jnp.sum(tot_all[...], axis=0)
@@ -534,7 +550,7 @@
 
     mark("p19_waitsend")
     left(wq_v.at[0], "w")
-    left(kvw_v.at[0], "w")
+    left(kv_v.at[0], "w")
     left(wo_v.at[0], "w")
     left(h_c.at[pl.ds(0, 7)], "a")
     left(gain_all.at[pl.ds(0, DP - 1)], "gain")
@@ -591,7 +607,8 @@
         scratch_shapes=[
             pltpu.VMEM((TEN, 16, 512), BF16),
             pltpu.VMEM((2, 512, 1024), BF16),
-            pltpu.VMEM((2, 512, 2, 128), BF16),
+            pltpu.VMEM((512, 2, 128), BF16),
+            pltpu.VMEM((2, 512, 256), BF16),
             pltpu.VMEM((16, 256, 128), BF16),
             pltpu.VMEM((16, 256, 128), BF16),
             pltpu.VMEM((2, 1024, 512), BF16),
@@ -617,6 +634,7 @@
             dma((9,)),
             dma((3,)),
             dma((4,)),
+            dma((4,)),
             dma((DP, 4)),
             dma((DP,)),
             dma((20,)),

time: 73.9 us -> 72.7 us (0.984)
  Pallas kernels: 72.1 us -> 70.9 us
    pallas_call x1, Pallas kernels: 72.1 us -> 70.9 us  [body(): pl.pallas_call(kernel, out_shape=jax.ShapeDtypeStruct((128, 512), F32), i...]
where the time goes in v4:
time: 72.7 us; the launch traced here: 72.5 us
  Pallas kernels  70.9 us (98%)
  local copies, waits for them, and re-layouts  1.67 us (2%)
    pallas_call x1, Pallas kernels, body(): pl.pallas_call(kernel, out_shape=jax.ShapeDtypeStruct((128, 512), F32), i...  70.9 us
    unnamed x1, local copies, waits for them, and re-layouts  1.67 us

profile of v4, /device:TPU:1, one launch (start us, length us, event | category | flops | bytes accessed | tf_op | source)
XLA Modules:
  0.0 72.5 jit_solution(8010500693051523804)
XLA Ops:
  0.0 70.9 %shard_map.109 = f32[128,512]{1,0:T(8,128)} custom-call(bf16[1,32,512]{2,1,0:T(8,128)(2,1)} %hidden.1, bf16[1,16,1,256,128]{4,3,2,1,0:T(8,128)(2,1)} %keys.1, bf16[1,16,1,256,128]{4,3,2,1,0:T(8,128)(2,1)} %vals.1, s32[1,16]{1,0:T(1,128)} %lens.1, s32[256,128]{1,0:T(8,128)} %ids.1, f32[2,128]{1,0:T(2,128)} %bitcast.1, bf16[512,1024]{1,0:T(8,128)(2,1)} %wq.1, ...), custom_call_target="tpu_custom_call" | custom-call | tf_op jit(solution)/shard_map/pallas_call | solution.py:590
  70.9 1.7 %copy.13 = f32[128,512]{1,0:T(8,128)} copy(f32[128,512]{1,0:T(8,128)} %shard_map.109) | data formatting | bytes 524288

commit v5 on v4

--- a/solution.py
+++ b/solution.py
@@ -152,6 +152,9 @@
     gcol,
     tot_one,
     tot_all,
+    gain_v,
+    lens_v,
+    guid_v,
     load_sem,
     w_recv,
     z_recv,
@@ -230,13 +233,16 @@
         return copy
 
     load(hidden.at[0, pl.ds(c * 16, 16)], h_c.at[T], recv_of["a"])
+    l_gain = load(gain, gain_v)
+    l_lens = load(lens, lens_v)
+    l_guid = load(guid, guid_v)
     l_wq = load(wq, wq_v.at[c])
     l_kv = load(kvw, kvw_v)
     for g in range(8):
         load(
             ids.at[pl.ds(S * 128 + PLACE[g] * 16, 16), :],
             ids_v.at[pl.ds(g * 16, 16), :],
-            load_sem.at[8],
+            load_sem.at[11],
         )
     l_k = load(keys.at[0, :, 0], k_v)
     l_v = load(vals.at[0, :, 0], v_v)
@@ -252,7 +258,8 @@
             )
     remote(hidden.at[0, pl.ds(16 - c * 16, 16)], h_c.at[T], send_of["a"], recv_of["a"], sib)
     remote(wq, wq_v.at[c], send_of["w"], w_recv.at[0], sib)
-    gain_all[D] = gain[...].astype(F32).reshape(1, 512)
+    l_gain.wait()
+    gain_all[D] = gain_v[...].astype(F32).reshape(1, 512)
     l_wh = load(wh, wh_v)
     remote(wo, wo_v.at[c], send_of["w"], w_recv.at[2], sib)
     l_kv.wait()
@@ -301,14 +308,16 @@
     lane = lax.broadcasted_iota(jnp.int32, (16, HEAD), 1)
     row = lax.broadcasted_iota(jnp.int32, (16, HEAD), 0)
     freq = jnp.exp(((lane % 64).astype(F32) * (2.0 / HEAD)) * (-jnp.log(F32(rope_theta))))
+    l_lens.wait()
+    l_guid.wait()
     position = jnp.zeros((16, HEAD), jnp.int32)
     for p in range(16):
-        position = jnp.where(row == p, lens[0, p], position)
+        position = jnp.where(row == p, lens_v[0, p], position)
     angle = position.astype(F32) * freq
     cosine = jnp.cos(angle)
     sine = jnp.sin(angle) * jnp.where(lane < 64, -1.0, 1.0)
 
-    pltpu.make_async_copy(ids.at[pl.ds(0, 128), :], ids_v, load_sem.at[8]).wait()
+    pltpu.make_async_copy(ids.at[pl.ds(0, 128), :], ids_v, load_sem.at[11]).wait()
     base = (D * TEN + T) * 512
     ids_v[...] = jnp.transpose(ids_v[...]) - base
     for n in range(4):
@@ -322,7 +331,7 @@
 
         total = lax.fori_loop(0, 16, add, jnp.zeros((128, 128), F32))
         counts[:, pl.ds(n * 128, 128)] = jnp.transpose(total) * penalty_step
-    guide = jnp.transpose(jnp.broadcast_to(guid[pl.ds(S, 1), :], (128, 128)))
+    guide = jnp.transpose(jnp.broadcast_to(guid_v[pl.ds(S, 1), :], (128, 128)))
     for g in range(8):
         gcol[g * 16 : (g + 1) * 16] = guide[PLACE[g] * 16 : (PLACE[g] + 1) * 16]
 
@@ -362,7 +371,7 @@
         e_own = jnp.exp(jnp.sum(q_all * k_own, axis=1, keepdims=True) * scale)
         e = jnp.concatenate(
             [
-                jnp.where(slot_at < lens[0, p], jnp.exp(scores[p - start] * scale), 0.0)
+                jnp.where(slot_at < lens_v[0, p], jnp.exp(scores[p - start] * scale), 0.0)
                 for p in prompts
             ]
         )
@@ -586,23 +595,10 @@
     dma = pltpu.SemaphoreType.DMA
     anywhere = pl.BlockSpec(memory_space=pl.ANY)
     vmem = pl.BlockSpec(memory_space=pltpu.VMEM)
-    smem = pl.BlockSpec(memory_space=pltpu.SMEM)
     return pl.pallas_call(
         kernel,
-        out_shape=jax.ShapeDtypeStruct((128, 512), F32),
-        in_specs=[
-            anywhere,
-            anywhere,
-            anywhere,
-            smem,
-            anywhere,
-            vmem,
-            anywhere,
-            anywhere,
-            anywhere,
-            vmem,
-            anywhere,
-        ],
+        out_shape=pltpu.VMEM((128, 512), F32),
+        in_specs=[anywhere] * 11,
         out_specs=vmem,
         scratch_shapes=[
             pltpu.VMEM((TEN, 16, 512), BF16),
@@ -631,7 +627,10 @@
             pltpu.VMEM((128, 128), F32),
             pltpu.VMEM((1, 128), F32),
             pltpu.VMEM((DP * TEN - 1, 1, 128), F32),
-            dma((9,)),
+            pltpu.VMEM((512,), BF16),
+            pltpu.SMEM((1, 16), jnp.int32),
+            pltpu.VMEM((2, 128), F32),
+            dma((12,)),
             dma((3,)),
             dma((4,)),
             dma((4,)),

time: 72.7 us -> 70.1 us (0.964)
  Pallas kernels: 70.9 us -> 69.3 us
  local copies, waits for them, and re-layouts: 1.67 us -> 0.71 us
    pallas_call x1, Pallas kernels: 70.9 us -> 69.3 us  [body(): pl.pallas_call(kernel, out_shape=pltpu.VMEM((128, 512), F32), in_specs=[a...]
    unnamed x1, local copies, waits for them, and re-layouts: 1.67 us -> 0.71 us
where the time goes in v5:
time: 70.1 us
  Pallas kernels  69.3 us (99%)
  local copies, waits for them, and re-layouts  0.71 us (1%)
    pallas_call x1, Pallas kernels, body(): pl.pallas_call(kernel, out_shape=pltpu.VMEM((128, 512), F32), in_specs=[a...  69.3 us

profile of v5, /device:TPU:1, one launch (start us, length us, event | category | flops | bytes accessed | tf_op | source)
XLA Modules:
  0.0 70.1 jit_solution(4266339877267203743)
XLA Ops:
  0.0 69.3 %shard_map.109 = f32[128,512]{1,0:T(8,128)S(1)} custom-call(bf16[1,32,512]{2,1,0:T(8,128)(2,1)} %hidden.1, bf16[1,16,1,256,128]{4,3,2,1,0:T(8,128)(2,1)} %keys.1, bf16[1,16,1,256,128]{4,3,2,1,0:T(8,128)(2,1)} %vals.1, s32[1,16]{1,0:T(1,128)} %lens.1, s32[256,128]{1,0:T(8,128)} %ids.1, f32[2,128]{1,0:T(2,128)} %bitcast.1, bf16[512,1024]{1,0:T(8,128)(2,1)} %wq.1, ...), custom_call_target="tpu_custom_call" | custom-call | tf_op jit(solution)/shard_map/pallas_call | solution.py:598
  69.3 0.7 %copy.13 = f32[128,512]{1,0:T(8,128)} copy(f32[128,512]{1,0:T(8,128)S(1)} %shard_map.109) | data formatting | bytes 524288

commit v6 on v5

--- a/solution.py
+++ b/solution.py
@@ -106,6 +106,21 @@
 
 
 ORDER = plan()
+
+
+def semaphores():
+    number = {}
+    keys = [piece if HOPS[piece] else piece[:2] for piece in ORDER]
+    for key in keys:
+        number.setdefault(key, len(number))
+    return {piece: number[key] for piece, key in zip(ORDER, keys)}, len(number)
+
+
+SEM, N_SEM = semaphores()
+LEAVES = {}
+for leaf in ORDER:
+    if not HOPS[leaf]:
+        LEAVES[leaf[:2]] = LEAVES.get(leaf[:2], 0) + 1
 FAR = (2, 1, 3, 0)
 PLANE = sorted(
     [(dx, dy) for dx in range(RING) for dy in range(RING)],
@@ -152,6 +167,7 @@
     gcol,
     tot_one,
     tot_all,
+    hid_v,
     gain_v,
     lens_v,
     guid_v,
@@ -209,18 +225,17 @@
 
     mark("p00_entry")
     barrier = pltpu.get_barrier_semaphore()
-    for i in range(1, DP):
-        pl.semaphore_signal(
-            barrier, inc=1, device_id=(S, (D + i) % DP, T), device_id_type=MESH
-        )
-        pl.semaphore_signal(
-            barrier, inc=1, device_id=(S, (D + i) % DP, zl * 2 + 1 - c), device_id_type=MESH
-        )
-    for i in range(1, 16):
-        other = (S * TEN + T + i) % 16
-        pl.semaphore_signal(
-            barrier, inc=1, device_id=(other // TEN, D, other % TEN), device_id_type=MESH
-        )
+
+    def greet(dev):
+        pl.semaphore_signal(barrier, inc=1, device_id=dev, device_id_type=MESH)
+
+    for t in range(TEN):
+        greet((1 - S, D, t))
+    for dx, dy in PLANE[:-1]:
+        greet((S, peer(dx, dy), T))
+        greet((S, peer(dx, dy), zl * 2 + 1 - c))
+    for i in range(1, TEN):
+        greet((S, D, (T + i) % TEN))
 
     loads = []
 
@@ -232,6 +247,7 @@
         copy.start()
         return copy
 
+    l_hid = load(hidden.at[0], hid_v)
     load(hidden.at[0, pl.ds(c * 16, 16)], h_c.at[T], recv_of["a"])
     l_gain = load(gain, gain_v)
     l_lens = load(lens, lens_v)
@@ -242,11 +258,12 @@
         load(
             ids.at[pl.ds(S * 128 + PLACE[g] * 16, 16), :],
             ids_v.at[pl.ds(g * 16, 16), :],
-            load_sem.at[11],
+            load_sem.at[12],
         )
     l_k = load(keys.at[0, :, 0], k_v)
     l_v = load(vals.at[0, :, 0], v_v)
     l_wo = load(wo, wo_v.at[c])
+    l_hid.wait()
     pl.semaphore_wait(barrier, 45)
 
     mark("p01_hidden")
@@ -254,9 +271,9 @@
         for core in (0, 1):
             dev = (S, D, ((zl + dz) % 4) * 2 + core)
             remote(
-                hidden.at[0, pl.ds(core * 16, 16)], h_c.at[T], send_of["a"], recv_of["a"], dev
+                hid_v.at[pl.ds(core * 16, 16)], h_c.at[T], send_of["a"], recv_of["a"], dev
             )
-    remote(hidden.at[0, pl.ds(16 - c * 16, 16)], h_c.at[T], send_of["a"], recv_of["a"], sib)
+    remote(hid_v.at[pl.ds(16 - c * 16, 16)], h_c.at[T], send_of["a"], recv_of["a"], sib)
     remote(wq, wq_v.at[c], send_of["w"], w_recv.at[0], sib)
     l_gain.wait()
     gain_all[D] = gain_v[...].astype(F32).reshape(1, 512)
@@ -317,7 +334,7 @@
     cosine = jnp.cos(angle)
     sine = jnp.sin(angle) * jnp.where(lane < 64, -1.0, 1.0)
 
-    pltpu.make_async_copy(ids.at[pl.ds(0, 128), :], ids_v, load_sem.at[11]).wait()
+    pltpu.make_async_copy(ids.at[pl.ds(0, 128), :], ids_v, load_sem.at[12]).wait()
     base = (D * TEN + T) * 512
     ids_v[...] = jnp.transpose(ids_v[...]) - base
     for n in range(4):
@@ -483,7 +500,7 @@
         slot, quarter = slot_of(*piece[:2]), piece[2]
         rows = buf.at[c, slot, pl.ds(quarter * 32, 32), :]
         for hop in hops:
-            remote(rows, rows, send_of["f"], f_recv.at[slot, quarter], neighbour(*hop))
+            remote(rows, rows, send_of["f"], f_recv.at[SEM[onward(piece, hop)]], neighbour(*hop))
 
     def share(dx, dy):
         whole = buf.at[c, slot_of(dx, dy)]
@@ -511,14 +528,19 @@
         send_on((0, 0, quarter), HOPS[(0, 0, quarter)][2:])
     share(0, 0)
     complete = [(0, (0, 0))]
-    held = {}
+    held, leaves = {}, {}
     for n, piece in enumerate(ORDER):
         if n % 10 == 0:
             mark(f"p12_pieces{n:02d}")
         dx, dy, quarter = piece
         slot = slot_of(dx, dy)
-        arrived(buf.at[c, slot, pl.ds(quarter * 32, 32), :], f_recv.at[slot, quarter])
-        send_on(piece, forwards(piece))
+        if HOPS[piece]:
+            arrived(buf.at[c, slot, pl.ds(quarter * 32, 32), :], f_recv.at[SEM[piece]])
+            send_on(piece, forwards(piece))
+        else:
+            leaves[dx, dy] = leaves.get((dx, dy), 0) + 1
+            if leaves[dx, dy] == LEAVES[dx, dy]:
+                arrived(buf.at[c, slot, pl.ds(0, 32 * LEAVES[dx, dy]), :], f_recv.at[SEM[piece]])
         held[dx, dy] = held.get((dx, dy), 0) + 1
         if held[dx, dy] == 4:
             share(dx, dy)
@@ -627,14 +649,15 @@
             pltpu.VMEM((128, 128), F32),
             pltpu.VMEM((1, 128), F32),
             pltpu.VMEM((DP * TEN - 1, 1, 128), F32),
+            pltpu.VMEM((32, 512), BF16),
             pltpu.VMEM((512,), BF16),
             pltpu.SMEM((1, 16), jnp.int32),
             pltpu.VMEM((2, 128), F32),
-            dma((12,)),
+            dma((13,)),
             dma((3,)),
             dma((4,)),
             dma((4,)),
-            dma((DP, 4)),
+            dma((N_SEM,)),
             dma((DP,)),
             dma((20,)),
         ],

time: 70.1 us -> 69.4 us (0.990)
    pallas_call x1, Pallas kernels: 69.3 us -> 68.6 us  [body(): pl.pallas_call(kernel, out_shape=pltpu.VMEM((128, 512), F32), in_specs=[a...]
where the time goes in v6:
time: 69.4 us; the launch traced here: 69.3 us
  Pallas kernels  68.6 us (99%)
  local copies, waits for them, and re-layouts  0.71 us (1%)
    pallas_call x1, Pallas kernels, body(): pl.pallas_call(kernel, out_shape=pltpu.VMEM((128, 512), F32), in_specs=[a...  68.6 us

profile of v6, /device:TPU:1, one launch (start us, length us, event | category | flops | bytes accessed | tf_op | source)
XLA Modules:
  0.0 69.3 jit_solution(6217224460487545348)
XLA Ops:
  0.0 68.6 %shard_map.109 = f32[128,512]{1,0:T(8,128)S(1)} custom-call(bf16[1,32,512]{2,1,0:T(8,128)(2,1)} %hidden.1, bf16[1,16,1,256,128]{4,3,2,1,0:T(8,128)(2,1)} %keys.1, bf16[1,16,1,256,128]{4,3,2,1,0:T(8,128)(2,1)} %vals.1, s32[1,16]{1,0:T(1,128)} %lens.1, s32[256,128]{1,0:T(8,128)} %ids.1, f32[2,128]{1,0:T(2,128)} %bitcast.1, bf16[512,1024]{1,0:T(8,128)(2,1)} %wq.1, ...), custom_call_target="tpu_custom_call" | custom-call | tf_op jit(solution)/shard_map/pallas_call | solution.py:620
  68.6 0.7 %copy.13 = f32[128,512]{1,0:T(8,128)} copy(f32[128,512]{1,0:T(8,128)S(1)} %shard_map.109) | data formatting | bytes 524288

commit v7 on v6

--- a/solution.py
+++ b/solution.py
@@ -185,9 +185,9 @@
     zl, c = T // 2, T % 2
     x, y = D // RING, D % RING
     sib = (S, D, zl * 2 + 1 - c)
-    names = ("w", "a", "gain", "b", "c", "d", "z", "f", "sib", "t")
-    send_of = {name: one.at[n] for n, name in enumerate(names)}
-    recv_of = {name: one.at[len(names) + n] for n, name in enumerate(names)}
+    names = ("a", "gain", "b", "c", "d", "t")
+    recv_of = {name: one.at[n] for n, name in enumerate(names)}
+    departed = one.at[len(names)]
 
     def remote(src, dst, ssem, rsem, dev):
         copy = pltpu.make_async_remote_copy(
@@ -204,18 +204,18 @@
         pltpu.make_async_remote_copy(
             src_ref=ref,
             dst_ref=ref,
-            send_sem=send_of["w"],
+            send_sem=departed,
             recv_sem=rsem,
             device_id=sib,
             device_id_type=MESH,
         ).wait_recv()
 
-    def left(ref, name):
+    def left(ref):
         pltpu.make_async_remote_copy(
             src_ref=ref,
             dst_ref=ref,
-            send_sem=send_of[name],
-            recv_sem=recv_of[name],
+            send_sem=departed,
+            recv_sem=recv_of["a"],
             device_id=sib,
             device_id_type=MESH,
         ).wait_send()
@@ -271,19 +271,19 @@
         for core in (0, 1):
             dev = (S, D, ((zl + dz) % 4) * 2 + core)
             remote(
-                hid_v.at[pl.ds(core * 16, 16)], h_c.at[T], send_of["a"], recv_of["a"], dev
+                hid_v.at[pl.ds(core * 16, 16)], h_c.at[T], departed, recv_of["a"], dev
             )
-    remote(hid_v.at[pl.ds(16 - c * 16, 16)], h_c.at[T], send_of["a"], recv_of["a"], sib)
-    remote(wq, wq_v.at[c], send_of["w"], w_recv.at[0], sib)
+    remote(hid_v.at[pl.ds(16 - c * 16, 16)], h_c.at[T], departed, recv_of["a"], sib)
+    remote(wq, wq_v.at[c], departed, w_recv.at[0], sib)
     l_gain.wait()
     gain_all[D] = gain_v[...].astype(F32).reshape(1, 512)
     l_wh = load(wh, wh_v)
-    remote(wo, wo_v.at[c], send_of["w"], w_recv.at[2], sib)
+    remote(wo, wo_v.at[c], departed, w_recv.at[2], sib)
     l_kv.wait()
     for n in range(2):
         kv_v[c, :, n * 128 : (n + 1) * 128] = kvw_v[:, n, :]
     l_wq.wait()
-    remote(kv_v.at[c], kv_v.at[c], send_of["w"], w_recv.at[1], sib)
+    remote(kv_v.at[c], kv_v.at[c], departed, w_recv.at[1], sib)
     arrived(h_c, recv_of["a"])
 
     mark("p02_qkv")
@@ -304,7 +304,7 @@
             k = to // 2
             if i == 1:
                 remote(
-                    part.at[k, g], recv_b.at[D], send_of["b"], recv_of["b"], (S, to, zl * 2 + g)
+                    part.at[k, g], recv_b.at[D], departed, recv_of["b"], (S, to, zl * 2 + g)
                 )
                 continue
 
@@ -315,11 +315,11 @@
             @pl.when(to != D)
             def _():
                 remote(
-                    part.at[k, g], recv_b.at[D], send_of["b"], recv_of["b"], (S, to, zl * 2 + g)
+                    part.at[k, g], recv_b.at[D], departed, recv_of["b"], (S, to, zl * 2 + g)
                 )
     for i in range(1, DP):
         to = (D + i) % DP
-        remote(gain_all.at[D], gain_all.at[D], send_of["gain"], recv_of["gain"], (S, to, T))
+        remote(gain_all.at[D], gain_all.at[D], departed, recv_of["gain"], (S, to, T))
 
     mark("p03_tables")
     lane = lax.broadcasted_iota(jnp.int32, (16, HEAD), 1)
@@ -415,7 +415,7 @@
     for dx, dy in PLANE:
         if (dx, dy) != (0, 0):
             to = peer(dx, dy)
-            remote(att_b, att_all.at[slot], send_of["c"], c_recv.at[x], (S, to, zl * 2 + core))
+            remote(att_b, att_all.at[slot], departed, c_recv.at[x], (S, to, zl * 2 + core))
 
     @pl.when(core == c)
     def _():
@@ -423,7 +423,7 @@
 
     @pl.when(core != c)
     def _():
-        remote(att_b, att_all.at[slot], send_of["c"], c_recv.at[x], sib)
+        remote(att_b, att_all.at[slot], departed, c_recv.at[x], sib)
 
     l_wo.wait()
     arrived(wo_v.at[1 - c], w_recv.at[2])
@@ -450,7 +450,7 @@
                 remote(
                     part_d.at[block],
                     recv_d.at[(zl - to + 3) % 4],
-                    send_of["d"],
+                    departed,
                     recv_of["d"],
                     (S, D, to * 2 + c),
                 )
@@ -481,7 +481,7 @@
 
         @pl.when(jnp.logical_not(at_home))
         def _():
-            remote(resid, place, send_of["z"], z_recv.at[my_j], (my_half, D, 2 * z + S))
+            remote(resid, place, departed, z_recv.at[my_j], (my_half, D, 2 * z + S))
 
     arrived(gain_all.at[pl.ds(0, DP - 1)], recv_of["gain"])
     l_wh.wait()
@@ -500,11 +500,11 @@
         slot, quarter = slot_of(*piece[:2]), piece[2]
         rows = buf.at[c, slot, pl.ds(quarter * 32, 32), :]
         for hop in hops:
-            remote(rows, rows, send_of["f"], f_recv.at[SEM[onward(piece, hop)]], neighbour(*hop))
+            remote(rows, rows, departed, f_recv.at[SEM[onward(piece, hop)]], neighbour(*hop))
 
     def share(dx, dy):
         whole = buf.at[c, slot_of(dx, dy)]
-        remote(whole, whole, send_of["sib"], sib_recv.at[slot_of(dx, dy)], sib)
+        remote(whole, whole, departed, sib_recv.at[slot_of(dx, dy)], sib)
 
     def head(dx, dy):
         slot = slot_of(dx, dy)
@@ -567,7 +567,7 @@
         for dt in range(TEN):
             if (dx, dy, dt) != (0, 0, 0):
                 to = (S, peer(dx, dy), (T + dt) % TEN)
-                remote(tot_one, tot_all.at[n * TEN + dt - n // 15], send_of["t"], recv_of["t"], to)
+                remote(tot_one, tot_all.at[n * TEN + dt - n // 15], departed, recv_of["t"], to)
     arrived(tot_all, recv_of["t"])
     mark("p18_out")
     totals = tot_one[...] + jnp.sum(tot_all[...], axis=0)
@@ -580,35 +580,35 @@
             )
 
     mark("p19_waitsend")
-    left(wq_v.at[0], "w")
-    left(kv_v.at[0], "w")
-    left(wo_v.at[0], "w")
-    left(h_c.at[pl.ds(0, 7)], "a")
-    left(gain_all.at[pl.ds(0, DP - 1)], "gain")
-    left(part_d.at[pl.ds(0, 3)], "d")
-    left(buf.at[0, pl.ds(0, 15)], "f")
-    left(buf.at[0], "sib")
-    left(tot_all, "t")
+    left(wq_v.at[0])
+    left(kv_v.at[0])
+    left(wo_v.at[0])
+    left(h_c.at[pl.ds(0, 7)])
+    left(gain_all.at[pl.ds(0, DP - 1)])
+    left(part_d.at[pl.ds(0, 3)])
+    left(buf.at[0, pl.ds(0, 15)])
+    left(buf.at[0])
+    left(tot_all)
     kept_c = core == c
     kept_z = jnp.logical_and(my_half == S, c == S)
 
     @pl.when(kept_c)
     def _():
-        left(recv_b.at[pl.ds(0, DP - 1)], "b")
-        left(att_all.at[pl.ds(0, DP - 1)], "c")
+        left(recv_b.at[pl.ds(0, DP - 1)])
+        left(att_all.at[pl.ds(0, DP - 1)])
 
     @pl.when(jnp.logical_not(kept_c))
     def _():
-        left(recv_b, "b")
-        left(att_all, "c")
+        left(recv_b)
+        left(att_all)
 
     @pl.when(kept_z)
     def _():
-        left(part_d.at[pl.ds(0, 3)], "z")
+        left(part_d.at[pl.ds(0, 3)])
 
     @pl.when(jnp.logical_not(kept_z))
     def _():
-        left(part_d, "z")
+        left(part_d)
 
     mark(None)
 
@@ -659,7 +659,7 @@
             dma((4,)),
             dma((N_SEM,)),
             dma((DP,)),
-            dma((20,)),
+            dma((7,)),
         ],
         compiler_params=pltpu.CompilerParams(
             collective_id=0, has_side_effects=True, vmem_limit_bytes=60 * 1024 * 1024

time: 69.4 us -> 69.2 us (level)
  no operation moved by 1% of the time
where the time goes in v7:
time: 69.2 us
  Pallas kernels  68.4 us (99%)
  local copies, waits for them, and re-layouts  0.71 us (1%)
    pallas_call x1, Pallas kernels, body(): pl.pallas_call(kernel, out_shape=pltpu.VMEM((128, 512), F32), in_specs=[a...  68.4 us

profile of v7, /device:TPU:1, one launch (start us, length us, event | category | flops | bytes accessed | tf_op | source)
XLA Modules:
  0.0 69.2 jit_solution(13362685003269739579)
XLA Ops:
  0.0 68.4 %shard_map.109 = f32[128,512]{1,0:T(8,128)S(1)} custom-call(bf16[1,32,512]{2,1,0:T(8,128)(2,1)} %hidden.1, bf16[1,16,1,256,128]{4,3,2,1,0:T(8,128)(2,1)} %keys.1, bf16[1,16,1,256,128]{4,3,2,1,0:T(8,128)(2,1)} %vals.1, s32[1,16]{1,0:T(1,128)} %lens.1, s32[256,128]{1,0:T(8,128)} %ids.1, f32[2,128]{1,0:T(2,128)} %bitcast.1, bf16[512,1024]{1,0:T(8,128)(2,1)} %wq.1, ...), custom_call_target="tpu_custom_call" | custom-call | tf_op jit(solution)/shard_map/pallas_call | solution.py:620
  68.4 0.7 %copy.13 = f32[128,512]{1,0:T(8,128)} copy(f32[128,512]{1,0:T(8,128)S(1)} %shard_map.109) | data formatting | bytes 524288

commit v8 on v7

--- a/solution.py
+++ b/solution.py
@@ -472,7 +472,8 @@
 
     mark("p10_z")
     place = buf.at[S, D, pl.ds(my_j * 32, 32), :]
-    for z in range(4):
+    for turn_z in (2, 1, 3, 0):
+        z = (zl + turn_z) % 4
         at_home = jnp.logical_and(my_half == S, 2 * z + S == T)
 
         @pl.when(at_home)

time: 69.2 us -> 69.1 us (level)
  no operation moved by 1% of the time
where the time goes in v8:
time: 69.1 us; the launch traced here: 69 us
  Pallas kernels  68.3 us (99%)
  local copies, waits for them, and re-layouts  0.71 us (1%)
    pallas_call x1, Pallas kernels, body(): pl.pallas_call(kernel, out_shape=pltpu.VMEM((128, 512), F32), in_specs=[a...  68.3 us

profile of v8, /device:TPU:1, one launch (start us, length us, event | category | flops | bytes accessed | tf_op | source)
XLA Modules:
  0.0 69.0 jit_solution(4738724628353144855)
XLA Ops:
  0.0 68.3 %shard_map.109 = f32[128,512]{1,0:T(8,128)S(1)} custom-call(bf16[1,32,512]{2,1,0:T(8,128)(2,1)} %hidden.1, bf16[1,16,1,256,128]{4,3,2,1,0:T(8,128)(2,1)} %keys.1, bf16[1,16,1,256,128]{4,3,2,1,0:T(8,128)(2,1)} %vals.1, s32[1,16]{1,0:T(1,128)} %lens.1, s32[256,128]{1,0:T(8,128)} %ids.1, f32[2,128]{1,0:T(2,128)} %bitcast.1, bf16[512,1024]{1,0:T(8,128)(2,1)} %wq.1, ...), custom_call_target="tpu_custom_call" | custom-call | tf_op jit(solution)/shard_map/pallas_call | solution.py:621
  68.3 0.7 %copy.13 = f32[128,512]{1,0:T(8,128)} copy(f32[128,512]{1,0:T(8,128)S(1)} %shard_map.109) | data formatting | bytes 524288
